TPU v7x, 256 devices: a whole 4x4x8 slice. The times are simulated.
256 devices in a mesh: dp: 128 (over z, y, x), mp: 2 (over core).
Axes of the slice: x: 4, y: 4, z: 8, core: 2. Of those that a mesh axis runs over, the one named last changes fastest.
Arguments:
- tokens: bfloat16 [16384, 4096], P('dp')
- key_cot: bfloat16 [16384, 1024], P('dp', 'mp'), may hold values from -6 to 6
- routes: int32 [16384, 1], P('dp'), may hold values from 0 to 127; in each aligned block of 128 rows (0 to 127, 128 to 255, ...) at most 2 rows name the same one
- counts: int32 [128, 4], P('dp'), may hold values from 1 to 64, 128 in all within a row
- widths: int32 [4], replicated, may hold values from 2 to 8, as said below
- key_weight: bfloat16 [4096, 1024], P('dp', 'mp')
Outputs:
- row_grads: bfloat16 [32768, 4096], P('dp', 'mp')
- key_grad: float32 [4096, 1024], P('dp', 'mp')
Inputs may be any that keep to these rules, and one draw needn't show every extreme that they name: `routes`: within the rows of one index of dp no destination is named more than 2 times, a bound that some block reaches. Each index of dp has 4 counts that sum to 128. widths[0] = 8 (the full net), widths[1] = 8 // 4 (the smallest), the other two lie strictly between.
All inputs are finite; a program needn't handle non-finite values.
Results may differ from a plain program's by a relative error of at most 0.0058.
Values may be sent and summed in bfloat16 or wider, within the bound.
A program may use at most 64 MiB of HBM per device.

v0:
```python
import math

import jax
import jax.numpy as jnp
from jax import lax
from jax.sharding import PartitionSpec as P

HEAD_DIM = 128
NSUB = 4


epsilon = 1e-06


def per_device(tokens, key_cot, routes, counts, widths, key_weight):
    row_count = tokens.shape[0]
    width_model = tokens.shape[1]
    local_cols = key_cot.shape[1]
    local_heads = local_cols // HEAD_DIM
    dp_size = lax.axis_size("dp")
    per_peer = 2 * row_count // dp_size
    receive = dp_size * per_peer
    destination = routes[:, 0]
    one_hot = (destination[:, None] == jnp.arange(dp_size, dtype=jnp.int32)[None, :]).astype(
        jnp.int32
    )
    earlier = jnp.sum(jnp.cumsum(one_hot, axis=0) * one_hot, axis=1) - 1
    send_slot = destination * per_peer + earlier
    bounds = jnp.cumsum(counts[0])
    positions = jnp.arange(row_count, dtype=jnp.int32)
    subnet = jnp.sum((positions[:, None] >= bounds[None, : NSUB - 1]).astype(jnp.int32), axis=1)
    send_subnet = (
        jnp.full((receive,), -1, jnp.int32).at[send_slot].set(subnet).reshape(dp_size, per_peer)
    )
    send_cot = jnp.zeros((receive, local_cols), jnp.bfloat16).at[send_slot].set(key_cot)
    send_cot = send_cot.reshape(dp_size, per_peer, local_cols)
    send_tokens = jnp.zeros((receive, width_model), jnp.bfloat16).at[send_slot].set(tokens)
    send_tokens = send_tokens.reshape(dp_size, per_peer, width_model)
    got_tokens, got_cot, got_subnet = (
        lax.all_to_all(send_tokens, "dp", split_axis=0, concat_axis=0, tiled=True),
        lax.all_to_all(send_cot, "dp", split_axis=0, concat_axis=0, tiled=True),
        lax.all_to_all(send_subnet, "dp", split_axis=0, concat_axis=0, tiled=True),
    )
    hidden = got_tokens.reshape(receive, width_model)
    got_cot = got_cot.reshape(receive, local_cols)
    got_subnet = got_subnet.reshape(receive)
    full_weight = lax.all_gather(key_weight, "dp", axis=0, tiled=True)
    key_proj = jnp.dot(hidden, full_weight, preferred_element_type=jnp.float32)
    per_head = key_proj.reshape(receive, local_heads, HEAD_DIM)
    head_scale = jnp.sqrt(jnp.mean(per_head * per_head, axis=2, keepdims=True) + epsilon)
    outputs = per_head / head_scale
    subnet_match = got_subnet[:, None] == jnp.arange(NSUB, dtype=jnp.int32)[None, :]
    row_width = jnp.sum(jnp.where(subnet_match, widths[None, :], 0), axis=1)
    head_index = lax.axis_index("mp") * local_heads + jnp.arange(local_heads, dtype=jnp.int32)
    head_mask = (head_index[None, :] < row_width[:, None]).astype(jnp.float32)
    upstream = (
        got_cot.astype(jnp.float32).reshape(receive, local_heads, HEAD_DIM) * head_mask[:, :, None]
    )
    key_delta = (
        upstream - outputs * jnp.mean(upstream * outputs, axis=2, keepdims=True)
    ) / head_scale
    delta_low = key_delta.reshape(receive, local_cols).astype(jnp.bfloat16)
    part_delta = lax.dot_general(
        delta_low, full_weight, (((1,), (1,)), ((), ())), preferred_element_type=jnp.float32
    )
    rounded = lax.optimization_barrier(part_delta.astype(jnp.bfloat16)).astype(jnp.float32)
    feature_delta = lax.psum_scatter(
        rounded.astype(jnp.bfloat16), "mp", scatter_dimension=1, tiled=True
    )
    weight_sum = lax.psum_scatter(
        lax.dot_general(
            hidden, delta_low, (((0,), (0,)), ((), ())), preferred_element_type=jnp.float32
        ),
        "dp",
        scatter_dimension=0,
        tiled=True,
    )
    key_grad = weight_sum / math.sqrt(row_count * dp_size)
    return (feature_delta, key_grad)


def solution(mesh):
    return jax.shard_map(
        per_device,
        mesh=mesh,
        in_specs=(P("dp", None), P("dp", "mp"), P("dp", None), P("dp", None), P(), P("dp", "mp")),
        out_specs=(P("dp", "mp"), P("dp", "mp")),
        check_vma=False,
    )
```

profile of v0, /device:TPU:2, one launch (start us, length us, event | category | flops | bytes accessed | tf_op | source)
XLA Modules:
  0.0 883.7 jit_solution(2644919228090402769)
XLA Ops:
  7.9 0.8 reduce-window.4
  9.7 0.8 select_reduce_fusion
  11.2 1.0 scatter_custom_fusion.1
  13.0 15.4 %all-to-all-start.1 = ((s32[128,1,2]{2,1,0:T(1,128)}), s32[128,1,2]{2,1,0:T(1,128)S(1)}, u32[]{:S(2)}, u32[]{:S(2)}) async-start(s32[128,1,2]{2,1,0:T(1,128)} %bitcast.5), calls=%async_computation.1 | async-start | bytes 131072 | tf_op jit(solution)/shard_map/all_to_all | solution.py:42
  28.4 1.5 scatter_custom_fusion
  30.7 8.9 %all-to-all-done.1 = s32[128,1,2]{2,1,0:T(1,128)S(1)} async-done(((s32[128,1,2]{2,1,0:T(1,128)}), s32[128,1,2]{2,1,0:T(1,128)S(1)}, u32[]{:S(2)}, u32[]{:S(2)}) %all-to-all-start.1) | async-done | bytes 1056 | tf_op jit(solution)/shard_map/all_to_all | solution.py:42
  39.7 6.6 all-to-all-start
  46.3 3.4 scatter_custom_fusion.2
  49.7 2.7 reshape.94
  52.4 7.6 all-to-all-done
  60.0 6.7 all-to-all-start.2
  67.4 0.8 reduce.3
  69.0 54.2 %all-to-all-done.2 = bf16[128,2,4096]{2,1,0:T(2,128)(2,1)S(1)} async-done(((bf16[128,2,4096]{2,1,0:T(2,128)(2,1)}), bf16[128,2,4096]{2,1,0:T(2,128)(2,1)S(1)}, u32[]{:S(2)}, u32[]{:S(2)}) %all-to-all-start.2) | async-done | bytes 2097184 | tf_op jit(solution)/shard_map/all_to_all | solution.py:40
  123.2 2.2 reshape.121
  125.4 2.2 reshape.95
  127.6 11.5 %all-gather.2.cloned.1.call-done = bf16[4096,512]{1,0:T(8,128)(2,1)} async-done(((bf16[32,512]{1,0:T(8,128)(2,1)}), bf16[4096,512]{1,0:T(8,128)(2,1)}) %all-gather.2.cloned.1.call-update) | async-done | bytes 4194320 | tf_op jit(solution)/shard_map/all_gather | solution.py:47
  139.1 6.6 copy.16
  145.7 3.5 multiply_reduce_fusion.1
  149.4 1.3 copy-done
  150.7 4.5 fusion.8
  155.3 4.9 convolution_convert_fusion
  160.2 699.1 %reduce-scatter.5.cloned.1.call-done = f32[32,512]{1,0:T(8,128)} async-done(((f32[4096,512]{1,0:T(8,128)}), f32[32,512]{1,0:T(8,128)}) %reduce-scatter.5.cloned.1.call-update) | async-done | bytes 65552 | tf_op jit(solution)/shard_map/reduce_scatter | solution.py:70
  859.4 1.5 broadcast_multiply_fusion
  860.8 16.3 %reduce-scatter.3.cloned.1.call-done = bf16[256,2048]{1,0:T(8,128)(2,1)} async-done(((bf16[256,4096]{1,0:T(8,128)(2,1)}), bf16[256,2048]{1,0:T(8,128)(2,1)}) %reduce-scatter.3.cloned.1.call-update) | async-done | bytes 1048592 | tf_op jit(solution)/shard_map/reduce_scatter | solution.py:67
  (29 shorter events, 5.7 us)
Async XLA Ops:
  7.2 131.9 %all-gather.2.cloned.1.call-start = ((), (), s32[]{:S(2)}) async-start(), calls=%async_computation.5 | async-start | bytes 4227072 | tf_op jit(solution)/shard_map/all_gather | solution.py:47
  13.0 26.7 %all-to-all-start.1 = ((s32[128,1,2]{2,1,0:T(1,128)}), s32[128,1,2]{2,1,0:T(1,128)S(1)}, u32[]{:S(2)}, u32[]{:S(2)}) async-start(s32[128,1,2]{2,1,0:T(1,128)} %bitcast.5), calls=%async_computation.1 | async-start | bytes 131072 | tf_op jit(solution)/shard_map/all_to_all | solution.py:42
  39.7 20.3 %all-to-all-start = ((bf16[128,2,512]{2,1,0:T(2,128)(2,1)}), bf16[128,2,512]{2,1,0:T(2,128)(2,1)S(1)}, u32[]{:S(2)}, u32[]{:S(2)}) async-start(bf16[128,2,512]{2,1,0:T(2,128)(2,1)} %reshape.92), calls=%async_computation | async-start | bytes 524288 | tf_op jit(solution)/shard_map/all_to_all | solution.py:41
  52.4 16.0 %copy-start.2 = (s32[4]{0:T(128)S(1)}, s32[4]{0:T(128)}, u32[]{:S(2)}) copy-start(s32[4]{0:T(128)} %param.10) | copy-start | bytes 52
  60.0 63.2 %all-to-all-start.2 = ((bf16[128,2,4096]{2,1,0:T(2,128)(2,1)}), bf16[128,2,4096]{2,1,0:T(2,128)(2,1)S(1)}, u32[]{:S(2)}, u32[]{:S(2)}) async-start(bf16[128,2,4096]{2,1,0:T(2,128)(2,1)} %reshape.94), calls=%async_computation.2 | async-start | bytes 4194304 | tf_op jit(solution)/shard_map/all_to_all | solution.py:40
  66.7 792.7 %reduce-scatter.5.cloned.1.call-start = ((), (), s32[]{:S(2)}) async-start(), calls=%async_computation.7 | async-start | bytes 8454144 | tf_op jit(solution)/shard_map/reduce_scatter | solution.py:70
  139.1 6.6 copy-start.1
  149.1 1.6 copy-start
  155.3 721.9 %reduce-scatter.3.cloned.1.call-start = ((), (), s32[]{:S(2)}) async-start(), calls=%async_computation.6 | async-start | bytes 3145728 | tf_op jit(solution)/shard_map/reduce_scatter | solution.py:67
Sparse Core Ops, SparseCore 0:
  11.6 127.4 all-gather.1
  155.4 703.9 reduce-scatter.4
  862.6 14.5 reduce-scatter.2
where the time goes:
time: 886 us; the launch traced here: 884 us
  waiting for transfers between devices  798 us (90%)
  starting transfers between devices  29 us (3%)
  local copies, waits for them, and re-layouts  23.6 us (3%)
  between operations  13.9 us (2%)
  matrix products  12.9 us (1%)
    reduce_scatter x1, waiting for transfers between devices, per_device(): lax.psum_scatter(lax.dot_general(hidden, delta_low, (((0,), (0,)), ((), (...  699 us
    all_to_all x1, waiting for transfers between devices, per_device(): lax.all_to_all(send_tokens, 'dp', split_axis=0, concat_axis=0, tiled=True)  54.2 us
  transfers between devices with their start and end apart: 6, of which 6 were waited for; matrix products, arithmetic and copies ran while one was open for 3% of the time, Pallas kernels for 0%

commit v1 on v0

v1 whole, which is shorter than its diff:
```python
import jax
import jax.numpy as jnp
from jax import lax
from jax.experimental import pallas as pl
from jax.experimental.pallas import tpu as pltpu
from jax.sharding import PartitionSpec as P

HEAD_DIM = 128
EPSILON = 1e-06
MESH = pl.DeviceIdType.MESH
NZ, NY, NX = 8, 4, 4
ROWS, WIDTH, COLS, FEATS = 128, 4096, 512, 32
HEADS = COLS // HEAD_DIM
A = (384, 512)
BC = (0, 384)
F32, BF16 = jnp.float32, jnp.bfloat16


def kernel(tokens, cot, routes, counts, widths, shard, rows_out, grad_out,
           W, tokT, dW, dl, D, S, R1, R2, R3, Rf, G, DXs, DXr,
           aZs, aZr, a1, aYs, aYr, a2, aXs, aXr,
           bXs, bXr, b1, bYs, bYr, cYs, cYr, c1, cXs, cXr, Zf, Zs, Zr,
           send_sem, recv_sem):
    me, m = lax.axis_index("dp"), lax.axis_index("mp")
    x, y, z = lax.rem(me, NX), lax.rem(me // NX, NY), me // (NX * NY)

    def device(zz, yy, xx, mm):
        return ((zz * NY + yy) * NX + xx, mm)

    def along(axis, j):
        return {"x": device(z, y, j, m), "y": device(z, j, x, m), "z": device(j, y, x, m)}[axis]

    place = {"x": (NX, x), "y": (NY, y), "z": (NZ, z)}

    def turn(axis, by):
        n, i = place[axis]
        return lax.rem(i + (by % n), n)

    copies = []

    def send(src, dst, to):
        at = len(copies)
        copy = pltpu.make_async_remote_copy(
            src_ref=src, dst_ref=dst, send_sem=send_sem.at[at], recv_sem=recv_sem.at[at],
            device_id=to, device_id_type=MESH)
        copy.start()
        copies.append(copy)
        return copy

    class Direct:
        def __init__(self, axis, src, dst):
            n, i = place[axis]
            self.sent = []
            for o in range(1, n):
                j = turn(axis, o)
                self.sent.append(send(src(j), dst(o), along(axis, j)))

        def wait(self):
            for copy in self.sent:
                copy.wait_recv()

    class Gather:
        def __init__(self, axis, region):
            self.axis, self.region, self.n = axis, region, place[axis][0]
            self.last = ()

        def wait(self):
            for copy in self.last:
                copy.wait_recv()

        def step(self, k):
            self.wait()
            halves = (0, 1) if k == self.n // 2 else (None, None)
            right = self.region(turn(self.axis, -(k - 1)), halves[0])
            left = self.region(turn(self.axis, k - 1), halves[1])
            self.last = (send(right, right, along(self.axis, turn(self.axis, 1))),
                         send(left, left, along(self.axis, turn(self.axis, -1))))

    class Reduce:
        def __init__(self, axis, lead, local, sbuf, rbuf):
            self.axis, self.lead, self.local, self.sbuf, self.rbuf = axis, lead, local, sbuf, rbuf
            self.n = place[axis][0]
            self.last = ()

        def step(self, t):
            n, lead = self.n, self.lead
            now = []
            for d in range(2):
                if t > 1:
                    self.last[d].wait_recv()
                by = n // 2 - t + 1
                j = turn(self.axis, by if d == 0 else -by)
                to = along(self.axis, turn(self.axis, 1 if d == 0 else -1))
                first, count = d * (lead // 2), lead // 2

                def plain(l, _):
                    self.sbuf[d, t - 1, l] = self.local(j, l).astype(BF16)
                    return 0

                def added(l, _):
                    self.sbuf[d, t - 1, l] = (self.local(j, l) + self.rbuf[d, t - 2, l].astype(F32)).astype(BF16)
                    return 0

                if t == 1:
                    lax.fori_loop(first, first + count, plain, 0)
                    part = pl.ds(first, count)
                    now.append(send(self.sbuf.at[d, t - 1, part], self.rbuf.at[d, t - 1, part], to))
                    continue
                if t == 2:
                    lax.fori_loop(first, first + count, added, 0)
                    lax.fori_loop(lead // 2 - first, lead - first, plain, 0)
                else:
                    lax.fori_loop(0, lead, added, 0)
                now.append(send(self.sbuf.at[d, t - 1], self.rbuf.at[d, t - 1], to))
            self.last = tuple(now)

        def finish(self, out):
            for copy in self.last:
                copy.wait_recv()
            i, s = place[self.axis][1], self.n // 2 - 1

            def body(l, _):
                out(l, self.local(i, l) + self.rbuf[0, s, l].astype(F32) + self.rbuf[1, s, l].astype(F32))
                return 0

            lax.fori_loop(0, self.lead, body, 0)

    barrier = pltpu.get_barrier_semaphore()
    peers = [along(axis, turn(axis, o)) for axis in "xyz" for o in range(1, place[axis][0])]
    peers.append(device(z, y, x, 1 - m))
    for peer in peers:
        pl.semaphore_signal(barrier, inc=1, device_id=peer, device_id_type=MESH)
    W[z, y, x] = shard[...]
    pl.semaphore_wait(barrier, len(peers))

    up, down = pl.ds(0, 16), pl.ds(16, 16)
    ca, cb = pl.ds(A[0], A[1] - A[0]), pl.ds(BC[0], BC[1] - BC[0])

    def zs(half):
        return pl.ds(0, NZ) if half is None else pl.ds(half * (NZ // 2), NZ // 2)

    def ys(half):
        return pl.ds(0, NY) if half is None else pl.ds(half * (NY // 2), NY // 2)

    every = pl.ds(0, NX)
    all_y = pl.ds(0, NY)
    own_bc = W.at[z, y, x, :, cb]
    bc_z = Direct("z", lambda j: own_bc, lambda o: own_bc)
    own_a = W.at[z, y, x, :, ca]
    a_x = Direct("x", lambda j: own_a, lambda o: own_a)

    def flip(s, _):
        cols = pl.ds(pl.multiple_of(s * 512, 512), 512)
        tokT[s] = tokens[:, cols].T
        return 0

    lax.fori_loop(0, 8, flip, 0)
    named = jnp.broadcast_to(routes[...], (ROWS, ROWS))
    first_index = lax.broadcasted_iota(jnp.int32, (ROWS, ROWS), 0)
    second_index = lax.broadcasted_iota(jnp.int32, (ROWS, ROWS), 1)
    same = (named == named.astype(F32).T.astype(jnp.int32)) & (first_index < second_index)
    earlier = jnp.sum(same.astype(F32), axis=0, keepdims=True).astype(jnp.int32)
    slot = (routes[...] * 2 + earlier) * HEADS

    a_x.wait()
    own_ay = W.at[z, y, every, :, ca]
    a_y = Direct("y", lambda j: own_ay, lambda o: own_ay)
    bc_z.wait()
    b_y = Gather("y", lambda j, h: W.at[zs(h), j, x, up, cb])
    c_x = Gather("x", lambda j, h: W.at[zs(h), y, j, down, cb])
    b_y.step(1)
    c_x.step(1)
    a_y.wait()
    a_z = Gather("z", lambda j, h: W.at[j, ys(h), every, :, ca])
    a_z.step(1)
    b_y.step(2)
    c_x.step(2)
    b_y.wait()
    b_x = Gather("x", lambda j, h: W.at[zs(h), all_y, j, up, cb])
    b_x.step(1)
    c_x.wait()
    c_y = Gather("y", lambda j, h: W.at[zs(h), j, every, down, cb])
    c_y.step(1)
    a_z.step(2)
    a_z.step(3)
    a_z.step(4)
    a_z.wait()

    position = lax.broadcasted_iota(jnp.int32, (ROWS, 1), 0)
    bound0 = counts[0, 0]
    bound1 = bound0 + counts[0, 1]
    bound2 = bound1 + counts[0, 2]
    row_width = jnp.where(position < bound0, widths[0], jnp.where(
        position < bound1, widths[1], jnp.where(position < bound2, widths[2], widths[3])))

    def grads(lo, hi):
        proj = jnp.zeros((ROWS, hi - lo), F32)
        for s in range(NZ):
            slab = W[s, :, :, :, lo:hi].reshape(512, hi - lo)
            proj += jnp.dot(tokens[:, s * 512:(s + 1) * 512], slab, preferred_element_type=F32)
        for h in range(lo // HEAD_DIM, hi // HEAD_DIM):
            cols = slice(h * HEAD_DIM, (h + 1) * HEAD_DIM)
            own = proj[:, h * HEAD_DIM - lo:(h + 1) * HEAD_DIM - lo]
            inverse = 1.0 / jnp.sqrt(jnp.mean(own * own, axis=1, keepdims=True) + EPSILON)
            outputs = own * inverse
            head_mask = (m * HEADS + h < row_width).astype(F32)
            upstream = cot[:, cols].astype(F32) * head_mask
            delta = (upstream - outputs * jnp.mean(upstream * outputs, axis=1, keepdims=True)) * inverse
            dl[:, cols] = delta.astype(BF16)
            D[h] = delta.astype(BF16)

        def term(s, _):
            part = jnp.dot(tokT[s], dl[:, lo:hi], preferred_element_type=F32)
            dW[s, :, :, :, lo:hi] = part.reshape(NY, NX, FEATS, hi - lo)
            return 0

        lax.fori_loop(0, NZ, term, 0)

    grads(*A)
    ra_z = Reduce("z", NY, lambda j, l: dW[j, l, :, :, A[0]:A[1]], aZs, aZr)
    ra_z.step(1)
    b_x.step(2)
    c_y.step(2)
    ra_z.step(2)
    b_x.wait()
    c_y.wait()
    grads(*BC)
    rb_x = Reduce("x", NZ, lambda j, l: dW[l, :, j, 0:16, BC[0]:BC[1]], bXs, bXr)
    rc_y = Reduce("y", NZ, lambda j, l: dW[l, j, :, 16:32, BC[0]:BC[1]], cYs, cYr)
    rb_x.step(1)
    rc_y.step(1)
    ra_z.step(3)

    def pack(s, _):
        at = lax.broadcasted_iota(jnp.int32, (ROWS, ROWS), 0) + s * ROWS
        total = jnp.zeros((ROWS, HEAD_DIM), F32)
        for h in range(HEADS):
            total += jnp.dot((at == slot + h).astype(F32).astype(BF16), D[h], preferred_element_type=F32)
        S[s] = total.reshape(NY, NX, 8, HEAD_DIM).astype(BF16)
        return 0

    lax.fori_loop(0, NZ, pack, 0)
    r_z = Direct("z", lambda j: S.at[j], lambda o: R1.at[z])
    R1[z] = S[z]
    ra_z.step(4)
    rb_x.step(2)
    rc_y.step(2)
    r_z.wait()
    all_z = pl.ds(0, NZ)
    r_y = Direct("y", lambda j: R1.at[all_z, j], lambda o: R2.at[all_z, y])

    def keep_y(s, _):
        R2[s, y] = R1[s, y]
        return 0

    lax.fori_loop(0, NZ, keep_y, 0)

    def put_a1(l, v):
        a1[l] = v

    ra_z.finish(put_a1)

    def cast_a1(l, _):
        aYs[l] = a1[l].astype(BF16)
        return 0

    lax.fori_loop(0, NY, cast_a1, 0)
    ra_y = Direct("y", lambda j: aYs.at[j], lambda o: aYr.at[o - 1])
    r_y.wait()
    r_x = Direct("x", lambda j: R2.at[all_z, all_y, j], lambda o: R3.at[all_z, all_y, x])

    def keep_x(s, _):
        R3[s, :, x] = R2[s, :, x]
        return 0

    lax.fori_loop(0, NZ, keep_x, 0)

    def put_b1(l, v):
        b1[l] = v

    def put_c1(l, v):
        c1[l] = v

    rb_x.finish(put_b1)
    rc_y.finish(put_c1)
    rb_y = Reduce("y", NZ, lambda j, l: b1[l, j], bYs, bYr)
    rc_x = Reduce("x", NZ, lambda j, l: c1[l, j], cXs, cXr)
    rb_y.step(1)
    rc_x.step(1)
    ra_y.wait()
    total = a1[y]
    for o in range(NY - 1):
        total += aYr[o].astype(F32)
    a2[...] = total
    aXs[...] = total.astype(BF16)
    ra_x = Direct("x", lambda j: aXs.at[j], lambda o: aXr.at[o - 1])

    r_x.wait()
    Rf[...] = R3[...].astype(F32).reshape(8 * ROWS, HEAD_DIM)
    for h in range(HEADS):
        G[:, h * HEAD_DIM:(h + 1) * HEAD_DIM] = Rf[pl.ds(h, 2 * ROWS, stride=HEADS), :].astype(BF16)

    def product(tile):
        return lax.dot_general(G[...], W[tile].reshape(512, COLS), (((1,), (1,)), ((), ())),
                               preferred_element_type=F32).astype(BF16)

    partner = device(z, y, x, 1 - m)
    halves = []
    for t in range(4):
        DXs[t] = product((1 - m) * 4 + t)
        halves.append(send(DXs.at[t], DXr.at[t], partner))
    rb_y.step(2)
    rc_x.step(2)
    for t in range(4):
        own = product(m * 4 + t).astype(F32)
        halves[t].wait_recv()
        rows_out[:, t * 512:(t + 1) * 512] = (own + DXr[t].astype(F32)).astype(BF16)

    ra_x.wait()
    total = a2[x]
    for o in range(NX - 1):
        total += aXr[o].astype(F32)
    scale = 1.0 / 128.0
    grad_out[:, A[0]:A[1]] = total * scale

    def put_b2(l, v):
        Zf[l, 0:16] = v

    def put_c2(l, v):
        Zf[l, 16:32] = v

    rb_y.finish(put_b2)
    rc_x.finish(put_c2)

    def cast_z(l, _):
        Zs[l] = Zf[l].astype(BF16)
        return 0

    lax.fori_loop(0, NZ, cast_z, 0)
    r_bc = Direct("z", lambda j: Zs.at[j], lambda o: Zr.at[o - 1])
    r_bc.wait()
    total = Zf[z]
    for o in range(NZ - 1):
        total += Zr[o].astype(F32)
    grad_out[:, BC[0]:BC[1]] = total * scale
    for copy in copies:
        copy.wait_send()


N_COPIES = 160


def per_device(tokens, key_cot, routes, counts, widths, key_weight):
    vmem = pl.BlockSpec(memory_space=pltpu.VMEM)
    smem = pl.BlockSpec(memory_space=pltpu.SMEM)
    buffers = [
        ((NZ, NY, NX, FEATS, COLS), BF16),
        ((8, 512, ROWS), BF16),
        ((NZ, NY, NX, FEATS, COLS), F32),
        ((ROWS, COLS), BF16),
        ((HEADS, ROWS, HEAD_DIM), BF16),
        ((NZ, NY, NX, 8, HEAD_DIM), BF16),
        ((NZ, NY, NX, 8, HEAD_DIM), BF16),
        ((NZ, NY, NX, 8, HEAD_DIM), BF16),
        ((NZ, NY, NX, 8, HEAD_DIM), BF16),
        ((8 * ROWS, HEAD_DIM), F32),
        ((2 * ROWS, COLS), BF16),
        ((4, 2 * ROWS, 512), BF16),
        ((4, 2 * ROWS, 512), BF16),
        ((2, 4, NY, NX, FEATS, 128), BF16),
        ((2, 4, NY, NX, FEATS, 128), BF16),
        ((NY, NX, FEATS, 128), F32),
        ((NY, NX, FEATS, 128), BF16),
        ((NY - 1, NX, FEATS, 128), BF16),
        ((NX, FEATS, 128), F32),
        ((NX, FEATS, 128), BF16),
        ((NX - 1, FEATS, 128), BF16),
        ((2, 2, NZ, NY, 16, 384), BF16),
        ((2, 2, NZ, NY, 16, 384), BF16),
        ((NZ, NY, 16, 384), F32),
        ((2, 2, NZ, 16, 384), BF16),
        ((2, 2, NZ, 16, 384), BF16),
        ((2, 2, NZ, NX, 16, 384), BF16),
        ((2, 2, NZ, NX, 16, 384), BF16),
        ((NZ, NX, 16, 384), F32),
        ((2, 2, NZ, 16, 384), BF16),
        ((2, 2, NZ, 16, 384), BF16),
        ((NZ, FEATS, 384), F32),
        ((NZ, FEATS, 384), BF16),
        ((NZ - 1, FEATS, 384), BF16),
    ]
    return pl.pallas_call(
        kernel,
        out_shape=(jax.ShapeDtypeStruct((2 * ROWS, WIDTH // 2), BF16), jax.ShapeDtypeStruct((FEATS, COLS), F32)),
        in_specs=[vmem, vmem, vmem, smem, smem, vmem],
        out_specs=(vmem, vmem),
        scratch_shapes=[pltpu.VMEM(shape, dtype) for shape, dtype in buffers]
        + [pltpu.SemaphoreType.DMA((N_COPIES,)), pltpu.SemaphoreType.DMA((N_COPIES,))],
        compiler_params=pltpu.CompilerParams(
            collective_id=0, has_side_effects=True, vmem_limit_bytes=58 << 20),
    )(tokens, key_cot, routes.reshape(1, ROWS), counts, widths, key_weight)


def solution(mesh):
    return jax.shard_map(
        per_device,
        mesh=mesh,
        in_specs=(P("dp", None), P("dp", "mp"), P("dp", None), P("dp", None), P(), P("dp", "mp")),
        out_specs=(P("dp", "mp"), P("dp", "mp")),
        check_vma=False,
    )
```

time: 886 us -> 93.9 us (0.11)
  waiting for transfers between devices: 798 us -> 0 us
  Pallas kernels: 0 us -> 89.9 us
  starting transfers between devices: 29 us -> 0 us
  local copies, waits for them, and re-layouts: 23.6 us -> 2.97 us
  between operations: 13.9 us -> 0.65 us
  matrix products: 12.9 us -> 0 us
    reduce_scatter x2 -> x0, waiting for transfers between devices: 715 us -> none  [the longest x1 699 us: per_device(): lax.psum_scatter(lax.dot_general(hidden, delta_low, (((0,), (0,)), ((), (...]
    pallas_call x0 -> x1, Pallas kernels: none -> 89.9 us  [per_device(): pl.pallas_call(kernel, out_shape=(jax.ShapeDtypeStruct((2 * ROWS, WIDTH /...]
    all_to_all x3 -> x0, waiting for transfers between devices: 70.7 us -> none  [the longest x1 54.2 us: per_device(): lax.all_to_all(send_tokens, 'dp', split_axis=0, concat_axis=0, tiled=True)]
    all_to_all x3 -> x0, starting transfers between devices: 28.7 us -> none  [the longest x1 15.4 us: per_device(): lax.all_to_all(send_subnet, 'dp', split_axis=0, concat_axis=0, tiled=True)]
    dot_general x3 -> x0, matrix products: 12.9 us -> none  [the longest x1 4.86 us: per_device(): lax.dot_general(delta_low, full_weight, (((1,), (1,)), ((), ())), preferr...]
    all_gather x1 -> x0, waiting for transfers between devices: 11.5 us -> none  [per_device(): full_weight = lax.all_gather(key_weight, 'dp', axis=0, tiled=True)]
  transfers between devices with their start and end apart: 6 -> 0, of which waited for: 6 -> 0; matrix products, arithmetic and copies ran while one was open for 3% -> 0% of each run, Pallas kernels for 0% -> 0%
where the time goes in v1:
time: 93.9 us; the launch traced here: 93.5 us
  Pallas kernels  89.9 us (96%)
  local copies, waits for them, and re-layouts  2.97 us (3%)
    pallas_call x1, Pallas kernels, per_device(): pl.pallas_call(kernel, out_shape=(jax.ShapeDtypeStruct((2 * ROWS, WIDTH /...  89.9 us
    unnamed x4, local copies, waits for them, and re-layouts  2.97 us

profile of v1, /device:TPU:2, one launch (start us, length us, event | category | flops | bytes accessed | tf_op | source)
XLA Modules:
  0.0 93.5 jit_solution(8817020536123633934)
XLA Ops:
  0.6 89.9 %shard_map.77 = (bf16[256,2048]{1,0:T(8,128)(2,1)}, f32[32,512]{1,0:T(8,128)}) custom-call(bf16[128,4096]{1,0:T(8,128)(2,1)} %tokens.1, bf16[128,512]{1,0:T(8,128)(2,1)} %cot.1, s32[1,128]{1,0:T(1,128)} %bitcast.1, s32[1,4]{1,0:T(1,128)} %counts.1, s32[4]{0:T(128)} %widths.1, bf16[32,512]{1,0:T(8,128)(2,1)} %shard.1), custom_call_target="tpu_custom_call" | custom-call | tf_op jit(solution)/shard_map/pallas_call | solution.py:392
  90.5 0.0 copy-start
  90.5 2.3 %copy.10 = bf16[256,2048]{1,0:T(8,128)(2,1)} copy(bf16[256,2048]{1,0:T(8,128)(2,1)} %get-tuple-element.4) | data formatting | bytes 2097152
  92.9 0.0 copy-done
  92.9 0.6 copy.11
Async XLA Ops:
  90.5 2.3 %copy-start = (f32[32,512]{1,0:T(8,128)S(1)}, f32[32,512]{1,0:T(8,128)}, u32[]{:S(2)}) copy-start(f32[32,512]{1,0:T(8,128)} %get-tuple-element.5) | copy-start | bytes 196612

commit v2 on v1

--- a/solution.py
+++ b/solution.py
@@ -17,7 +17,7 @@
 
 
 def kernel(tokens, cot, routes, counts, widths, shard, rows_out, grad_out,
-           W, tokT, dW, dl, D, S, R1, R2, R3, Rf, G, DXs, DXr,
+           W, tokT, dW, dl, D, S, R1, R3, Rf, G, DXs, DXr,
            aZs, aZr, a1, aYs, aYr, a2, aXs, aXr,
            bXs, bXr, b1, bYs, bYr, cYs, cYr, c1, cXs, cXr, Zf, Zs, Zr,
            send_sem, recv_sem):
@@ -81,6 +81,12 @@
             self.axis, self.lead, self.local, self.sbuf, self.rbuf = axis, lead, local, sbuf, rbuf
             self.n = place[axis][0]
             self.last = ()
+
+        def put(self, d, t, j, lo, hi, arrived):
+            value = self.local(j, lo, hi)
+            if arrived:
+                value += self.rbuf[d, t - 2, lo:hi].astype(F32)
+            self.sbuf[d, t - 1, lo:hi] = value.astype(BF16)
 
         def step(self, t):
             n, lead = self.n, self.lead
@@ -91,39 +97,27 @@
                 by = n // 2 - t + 1
                 j = turn(self.axis, by if d == 0 else -by)
                 to = along(self.axis, turn(self.axis, 1 if d == 0 else -1))
-                first, count = d * (lead // 2), lead // 2
-
-                def plain(l, _):
-                    self.sbuf[d, t - 1, l] = self.local(j, l).astype(BF16)
-                    return 0
-
-                def added(l, _):
-                    self.sbuf[d, t - 1, l] = (self.local(j, l) + self.rbuf[d, t - 2, l].astype(F32)).astype(BF16)
-                    return 0
-
+                half = lead // 2
+                first = d * half
                 if t == 1:
-                    lax.fori_loop(first, first + count, plain, 0)
-                    part = pl.ds(first, count)
+                    self.put(d, t, j, first, first + half, False)
+                    part = pl.ds(first, half)
                     now.append(send(self.sbuf.at[d, t - 1, part], self.rbuf.at[d, t - 1, part], to))
                     continue
                 if t == 2:
-                    lax.fori_loop(first, first + count, added, 0)
-                    lax.fori_loop(lead // 2 - first, lead - first, plain, 0)
+                    self.put(d, t, j, first, first + half, True)
+                    self.put(d, t, j, half - first, lead - first, False)
                 else:
-                    lax.fori_loop(0, lead, added, 0)
+                    for lo in range(0, lead, half):
+                        self.put(d, t, j, lo, lo + half, True)
                 now.append(send(self.sbuf.at[d, t - 1], self.rbuf.at[d, t - 1], to))
             self.last = tuple(now)
 
-        def finish(self, out):
+        def finish(self):
             for copy in self.last:
                 copy.wait_recv()
             i, s = place[self.axis][1], self.n // 2 - 1
-
-            def body(l, _):
-                out(l, self.local(i, l) + self.rbuf[0, s, l].astype(F32) + self.rbuf[1, s, l].astype(F32))
-                return 0
-
-            lax.fori_loop(0, self.lead, body, 0)
+            return (self.local(i, 0, self.lead) + self.rbuf[0, s].astype(F32)) + self.rbuf[1, s].astype(F32)
 
     barrier = pltpu.get_barrier_semaphore()
     peers = [along(axis, turn(axis, o)) for axis in "xyz" for o in range(1, place[axis][0])]
@@ -135,26 +129,56 @@
 
     up, down = pl.ds(0, 16), pl.ds(16, 16)
     ca, cb = pl.ds(A[0], A[1] - A[0]), pl.ds(BC[0], BC[1] - BC[0])
-
-    def zs(half):
-        return pl.ds(0, NZ) if half is None else pl.ds(half * (NZ // 2), NZ // 2)
-
-    def ys(half):
-        return pl.ds(0, NY) if half is None else pl.ds(half * (NY // 2), NY // 2)
-
     every = pl.ds(0, NX)
     all_y = pl.ds(0, NY)
+
+    def span(half, n=4):
+        return pl.ds(0, n) if half is None else pl.ds(half * (n // 2), n // 2)
+
+    class ChunkGather:
+        def __init__(self, q):
+            self.q = q
+
+        def near(self):
+            q = self.q
+            b_own, c_own = W.at[q, y, x, up, cb], W.at[q, y, x, down, cb]
+            self.b = Direct("y", lambda j: b_own, lambda o: b_own)
+            self.c = Direct("x", lambda j: c_own, lambda o: c_own)
+
+        def far(self, k):
+            q = self.q
+            if k == 1:
+                self.b.wait()
+                self.b = Gather("x", lambda j, h: W.at[q, span(h), j, up, cb])
+            self.b.step(k)
+            if k == 1:
+                self.c.wait()
+                self.c = Gather("y", lambda j, h: W.at[q, j, span(h), down, cb])
+            self.c.step(k)
+
+        def wait(self):
+            self.b.wait()
+            self.c.wait()
+
     own_bc = W.at[z, y, x, :, cb]
     bc_z = Direct("z", lambda j: own_bc, lambda o: own_bc)
+    chunks = [ChunkGather(turn("z", -o)) for o in range(NZ)]
+    chunks[0].near()
     own_a = W.at[z, y, x, :, ca]
     a_x = Direct("x", lambda j: own_a, lambda o: own_a)
 
-    def flip(s, _):
-        cols = pl.ds(pl.multiple_of(s * 512, 512), 512)
-        tokT[s] = tokens[:, cols].T
-        return 0
-
-    lax.fori_loop(0, 8, flip, 0)
+    def arrive(*offsets):
+        for o in offsets:
+            bc_z.sent[o - 1].wait_recv()
+            chunks[o].near()
+
+    def far(k, *offsets):
+        for o in offsets:
+            chunks[o].far(k)
+
+    def flip(s):
+        tokT[s] = tokens[:, s * 512:(s + 1) * 512].T
+
     named = jnp.broadcast_to(routes[...], (ROWS, ROWS))
     first_index = lax.broadcasted_iota(jnp.int32, (ROWS, ROWS), 0)
     second_index = lax.broadcasted_iota(jnp.int32, (ROWS, ROWS), 1)
@@ -162,29 +186,52 @@
     earlier = jnp.sum(same.astype(F32), axis=0, keepdims=True).astype(jnp.int32)
     slot = (routes[...] * 2 + earlier) * HEADS
 
+    def a_ring(oy):
+        row = turn("y", -oy)
+        return Gather("z", lambda j, h: W.at[j, row, span(h), :, ca])
+
+    a_rings = [a_ring(oy) for oy in range(NY)]
+
+    def a_far(k, *rings):
+        for oy in rings:
+            a_rings[oy].step(k)
+
     a_x.wait()
     own_ay = W.at[z, y, every, :, ca]
     a_y = Direct("y", lambda j: own_ay, lambda o: own_ay)
-    bc_z.wait()
-    b_y = Gather("y", lambda j, h: W.at[zs(h), j, x, up, cb])
-    c_x = Gather("x", lambda j, h: W.at[zs(h), y, j, down, cb])
-    b_y.step(1)
-    c_x.step(1)
+    a_far(1, 0)
+    far(1, 0)
+    arrive(1, 7)
+    flip(0)
+    arrive(2, 6)
     a_y.wait()
-    a_z = Gather("z", lambda j, h: W.at[j, ys(h), every, :, ca])
-    a_z.step(1)
-    b_y.step(2)
-    c_x.step(2)
-    b_y.wait()
-    b_x = Gather("x", lambda j, h: W.at[zs(h), all_y, j, up, cb])
-    b_x.step(1)
-    c_x.wait()
-    c_y = Gather("y", lambda j, h: W.at[zs(h), j, every, down, cb])
-    c_y.step(1)
-    a_z.step(2)
-    a_z.step(3)
-    a_z.step(4)
-    a_z.wait()
+    a_far(1, 1, 2, 3)
+    far(1, 1, 7)
+    arrive(3, 5)
+    a_far(2, 0)
+    far(2, 0)
+    arrive(4)
+    far(1, 2, 6)
+    flip(1)
+    a_far(2, 1, 2, 3)
+    far(2, 1, 7)
+    far(1, 3, 5)
+    flip(2)
+    a_far(3, 0)
+    far(2, 2, 6)
+    far(1, 4)
+    flip(3)
+    a_far(3, 1, 2, 3)
+    a_far(4, 0)
+    far(2, 3, 5)
+    flip(4)
+    flip(5)
+    far(2, 4)
+    flip(6)
+    flip(7)
+    a_far(4, 1, 2, 3)
+    for ring in a_rings:
+        ring.wait()
 
     position = lax.broadcasted_iota(jnp.int32, (ROWS, 1), 0)
     bound0 = counts[0, 0]
@@ -217,19 +264,52 @@
         lax.fori_loop(0, NZ, term, 0)
 
     grads(*A)
-    ra_z = Reduce("z", NY, lambda j, l: dW[j, l, :, :, A[0]:A[1]], aZs, aZr)
+    ra_z = Reduce("z", NY, lambda j, lo, hi: dW[j, lo:hi, :, :, A[0]:A[1]], aZs, aZr)
     ra_z.step(1)
-    b_x.step(2)
-    c_y.step(2)
-    ra_z.step(2)
-    b_x.wait()
-    c_y.wait()
+    for chunk in chunks:
+        chunk.wait()
     grads(*BC)
-    rb_x = Reduce("x", NZ, lambda j, l: dW[l, :, j, 0:16, BC[0]:BC[1]], bXs, bXr)
-    rc_y = Reduce("y", NZ, lambda j, l: dW[l, j, :, 16:32, BC[0]:BC[1]], cYs, cYr)
-    rb_x.step(1)
-    rc_y.step(1)
-    ra_z.step(3)
+
+    class ChunkReduce:
+        def __init__(self, at, o):
+            q = turn("z", -o)
+            self.at, self.o, self.q = at, o, q
+            self.b = Reduce("x", NY, lambda j, lo, hi: dW[q, lo:hi, j, 0:16, BC[0]:BC[1]], bXs.at[at], bXr.at[at])
+            self.c = Reduce("y", NX, lambda j, lo, hi: dW[q, j, lo:hi, 16:32, BC[0]:BC[1]], cYs.at[at], cYr.at[at])
+
+        def step(self, t):
+            self.b.step(t)
+            self.c.step(t)
+
+        def near(self):
+            at = self.at
+            total = self.b.finish()
+            b1[at] = total
+            bYs[at] = total.astype(BF16)
+            self.b = Direct("y", lambda j: bYs.at[at, j], lambda o: bYr.at[at, o - 1])
+            total = self.c.finish()
+            c1[at] = total
+            cXs[at] = total.astype(BF16)
+            self.c = Direct("x", lambda j: cXs.at[at, j], lambda o: cXr.at[at, o - 1])
+
+        def across(self):
+            at = self.at
+            for part, mine, arrived, rows, i in ((self.b, b1, bYr, slice(0, 16), y), (self.c, c1, cXr, slice(16, 32), x)):
+                part.wait()
+                total = mine[at, i]
+                for k in range(3):
+                    total += arrived[at, k].astype(F32)
+                if self.o == 0:
+                    Zf[rows] = total
+                else:
+                    Zs[at, rows] = total.astype(BF16)
+            if self.o:
+                self.sent = send(Zs.at[at], Zr.at[self.o - 1], along("z", self.q))
+
+    order = (4, 3, 5, 2, 6, 1, 7, 0)
+    units = [ChunkReduce(at, o) for at, o in enumerate(order)]
+    for unit in units[:4]:
+        unit.step(1)
 
     def pack(s, _):
         at = lax.broadcasted_iota(jnp.int32, (ROWS, ROWS), 0) + s * ROWS
@@ -242,51 +322,80 @@
     lax.fori_loop(0, NZ, pack, 0)
     r_z = Direct("z", lambda j: S.at[j], lambda o: R1.at[z])
     R1[z] = S[z]
-    ra_z.step(4)
-    rb_x.step(2)
-    rc_y.step(2)
+    for unit in units[4:]:
+        unit.step(1)
+    ra_z.step(2)
+    units[0].step(2)
+    units[1].step(2)
+    units[2].step(2)
+    units[3].step(2)
     r_z.wait()
     all_z = pl.ds(0, NZ)
-    r_y = Direct("y", lambda j: R1.at[all_z, j], lambda o: R2.at[all_z, y])
-
-    def keep_y(s, _):
-        R2[s, y] = R1[s, y]
+    r_xy = []
+    for oy in range(NY):
+        for ox in range(NX):
+            if oy or ox:
+                jy, jx = turn("y", oy), turn("x", ox)
+                r_xy.append(send(R1.at[all_z, jy, jx], R3.at[all_z, y, x], device(z, jy, jx, m)))
+
+    def keep(s, _):
+        R3[s, y, x] = R1[s, y, x]
         return 0
 
-    lax.fori_loop(0, NZ, keep_y, 0)
-
-    def put_a1(l, v):
-        a1[l] = v
-
-    ra_z.finish(put_a1)
-
-    def cast_a1(l, _):
-        aYs[l] = a1[l].astype(BF16)
-        return 0
-
-    lax.fori_loop(0, NY, cast_a1, 0)
+    lax.fori_loop(0, NZ, keep, 0)
+    units[0].near()
+    units[4].step(2)
+    ra_z.step(3)
+    units[1].near()
+    units[5].step(2)
+    units[2].near()
+    units[6].step(2)
+    units[0].across()
+    units[3].near()
+    units[7].step(2)
+    units[1].across()
+    ra_z.step(4)
+    units[4].near()
+    units[2].across()
+
+    for copy in r_xy:
+        copy.wait_recv()
+    Rf[...] = R3[...].astype(F32).reshape(8 * ROWS, HEAD_DIM)
+    for h in range(HEADS):
+        G[:, h * HEAD_DIM:(h + 1) * HEAD_DIM] = Rf[pl.ds(h, 2 * ROWS, stride=HEADS), :].astype(BF16)
+
+    def product(tile):
+        return lax.dot_general(G[...], W[tile].reshape(512, COLS), (((1,), (1,)), ((), ())),
+                               preferred_element_type=F32).astype(BF16)
+
+    partner = device(z, y, x, 1 - m)
+    halves = []
+
+    def give(t):
+        DXs[t] = product((1 - m) * 4 + t)
+        halves.append(send(DXs.at[t], DXr.at[t], partner))
+
+    def take(t):
+        own = product(m * 4 + t).astype(F32)
+        halves[t].wait_recv()
+        rows_out[:, t * 512:(t + 1) * 512] = (own + DXr[t].astype(F32)).astype(BF16)
+
+    give(0)
+    units[5].near()
+    units[3].across()
+    give(1)
+    units[6].near()
+    units[4].across()
+    total = ra_z.finish()
+    a1[...] = total
+    aYs[...] = total.astype(BF16)
     ra_y = Direct("y", lambda j: aYs.at[j], lambda o: aYr.at[o - 1])
-    r_y.wait()
-    r_x = Direct("x", lambda j: R2.at[all_z, all_y, j], lambda o: R3.at[all_z, all_y, x])
-
-    def keep_x(s, _):
-        R3[s, :, x] = R2[s, :, x]
-        return 0
-
-    lax.fori_loop(0, NZ, keep_x, 0)
-
-    def put_b1(l, v):
-        b1[l] = v
-
-    def put_c1(l, v):
-        c1[l] = v
-
-    rb_x.finish(put_b1)
-    rc_y.finish(put_c1)
-    rb_y = Reduce("y", NZ, lambda j, l: b1[l, j], bYs, bYr)
-    rc_x = Reduce("x", NZ, lambda j, l: c1[l, j], cXs, cXr)
-    rb_y.step(1)
-    rc_x.step(1)
+    units[7].near()
+    units[5].across()
+    give(2)
+    units[6].across()
+    give(3)
+    units[7].across()
     ra_y.wait()
     total = a1[y]
     for o in range(NY - 1):
@@ -294,60 +403,25 @@
     a2[...] = total
     aXs[...] = total.astype(BF16)
     ra_x = Direct("x", lambda j: aXs.at[j], lambda o: aXr.at[o - 1])
-
-    r_x.wait()
-    Rf[...] = R3[...].astype(F32).reshape(8 * ROWS, HEAD_DIM)
-    for h in range(HEADS):
-        G[:, h * HEAD_DIM:(h + 1) * HEAD_DIM] = Rf[pl.ds(h, 2 * ROWS, stride=HEADS), :].astype(BF16)
-
-    def product(tile):
-        return lax.dot_general(G[...], W[tile].reshape(512, COLS), (((1,), (1,)), ((), ())),
-                               preferred_element_type=F32).astype(BF16)
-
-    partner = device(z, y, x, 1 - m)
-    halves = []
     for t in range(4):
-        DXs[t] = product((1 - m) * 4 + t)
-        halves.append(send(DXs.at[t], DXr.at[t], partner))
-    rb_y.step(2)
-    rc_x.step(2)
-    for t in range(4):
-        own = product(m * 4 + t).astype(F32)
-        halves[t].wait_recv()
-        rows_out[:, t * 512:(t + 1) * 512] = (own + DXr[t].astype(F32)).astype(BF16)
-
+        take(t)
+    scale = 1.0 / 128.0
+    total = Zf[...]
+    for unit in units:
+        if unit.o:
+            unit.sent.wait_recv()
+            total += Zr[unit.o - 1].astype(F32)
+    grad_out[:, BC[0]:BC[1]] = total * scale
     ra_x.wait()
     total = a2[x]
     for o in range(NX - 1):
         total += aXr[o].astype(F32)
-    scale = 1.0 / 128.0
     grad_out[:, A[0]:A[1]] = total * scale
-
-    def put_b2(l, v):
-        Zf[l, 0:16] = v
-
-    def put_c2(l, v):
-        Zf[l, 16:32] = v
-
-    rb_y.finish(put_b2)
-    rc_x.finish(put_c2)
-
-    def cast_z(l, _):
-        Zs[l] = Zf[l].astype(BF16)
-        return 0
-
-    lax.fori_loop(0, NZ, cast_z, 0)
-    r_bc = Direct("z", lambda j: Zs.at[j], lambda o: Zr.at[o - 1])
-    r_bc.wait()
-    total = Zf[z]
-    for o in range(NZ - 1):
-        total += Zr[o].astype(F32)
-    grad_out[:, BC[0]:BC[1]] = total * scale
     for copy in copies:
         copy.wait_send()
 
 
-N_COPIES = 160
+N_COPIES = 400
 
 
 def per_device(tokens, key_cot, routes, counts, widths, key_weight):
@@ -359,7 +433,6 @@
         ((NZ, NY, NX, FEATS, COLS), F32),
         ((ROWS, COLS), BF16),
         ((HEADS, ROWS, HEAD_DIM), BF16),
-        ((NZ, NY, NX, 8, HEAD_DIM), BF16),
         ((NZ, NY, NX, 8, HEAD_DIM), BF16),
         ((NZ, NY, NX, 8, HEAD_DIM), BF16),
         ((NZ, NY, NX, 8, HEAD_DIM), BF16),
@@ -375,17 +448,17 @@
         ((NX, FEATS, 128), F32),
         ((NX, FEATS, 128), BF16),
         ((NX - 1, FEATS, 128), BF16),
-        ((2, 2, NZ, NY, 16, 384), BF16),
-        ((2, 2, NZ, NY, 16, 384), BF16),
+        ((NZ, 2, 2, NY, 16, 384), BF16),
+        ((NZ, 2, 2, NY, 16, 384), BF16),
         ((NZ, NY, 16, 384), F32),
-        ((2, 2, NZ, 16, 384), BF16),
-        ((2, 2, NZ, 16, 384), BF16),
-        ((2, 2, NZ, NX, 16, 384), BF16),
-        ((2, 2, NZ, NX, 16, 384), BF16),
+        ((NZ, NY, 16, 384), BF16),
+        ((NZ, NY - 1, 16, 384), BF16),
+        ((NZ, 2, 2, NX, 16, 384), BF16),
+        ((NZ, 2, 2, NX, 16, 384), BF16),
         ((NZ, NX, 16, 384), F32),
-        ((2, 2, NZ, 16, 384), BF16),
-        ((2, 2, NZ, 16, 384), BF16),
-        ((NZ, FEATS, 384), F32),
+        ((NZ, NX, 16, 384), BF16),
+        ((NZ, NX - 1, 16, 384), BF16),
+        ((FEATS, 384), F32),
         ((NZ, FEATS, 384), BF16),
         ((NZ - 1, FEATS, 384), BF16),
     ]

time: 93.9 us -> 83.1 us (0.88)
  Pallas kernels: 89.9 us -> 79.3 us
    pallas_call x1, Pallas kernels: 89.9 us -> 79.3 us  [per_device(): pl.pallas_call(kernel, out_shape=(jax.ShapeDtypeStruct((2 * ROWS, WIDTH /...]
where the time goes in v2:
time: 83.1 us; the launch traced here: 82.9 us
  Pallas kernels  79.3 us (95%)
  local copies, waits for them, and re-layouts  2.97 us (4%)
    pallas_call x1, Pallas kernels, per_device(): pl.pallas_call(kernel, out_shape=(jax.ShapeDtypeStruct((2 * ROWS, WIDTH /...  79.3 us
    unnamed x4, local copies, waits for them, and re-layouts  2.97 us

profile of v2, /device:TPU:2, one launch (start us, length us, event | category | flops | bytes accessed | tf_op | source)
XLA Modules:
  0.0 82.9 jit_solution(1893950927119585385)
XLA Ops:
  0.6 79.3 %shard_map.77 = (bf16[256,2048]{1,0:T(8,128)(2,1)}, f32[32,512]{1,0:T(8,128)}) custom-call(bf16[128,4096]{1,0:T(8,128)(2,1)} %tokens.1, bf16[128,512]{1,0:T(8,128)(2,1)} %cot.1, s32[1,128]{1,0:T(1,128)} %bitcast.1, s32[1,4]{1,0:T(1,128)} %counts.1, s32[4]{0:T(128)} %widths.1, bf16[32,512]{1,0:T(8,128)(2,1)} %shard.1), custom_call_target="tpu_custom_call" | custom-call | tf_op jit(solution)/shard_map/pallas_call | solution.py:465
  80.0 0.0 copy-start
  80.0 2.3 %copy.10 = bf16[256,2048]{1,0:T(8,128)(2,1)} copy(bf16[256,2048]{1,0:T(8,128)(2,1)} %get-tuple-element.4) | data formatting | bytes 2097152
  82.3 0.0 copy-done
  82.3 0.6 copy.11
Async XLA Ops:
  80.0 2.3 %copy-start = (f32[32,512]{1,0:T(8,128)S(1)}, f32[32,512]{1,0:T(8,128)}, u32[]{:S(2)}) copy-start(f32[32,512]{1,0:T(8,128)} %get-tuple-element.5) | copy-start | bytes 196612

commit v3 on v2

v3 whole, which is shorter than its diff:
```python
import math

import jax
import jax.numpy as jnp
from jax import lax
from jax.experimental import pallas as pl
from jax.experimental.pallas import tpu as pltpu
from jax.sharding import PartitionSpec as P

HEAD_DIM = 128
EPSILON = 1e-06
MESH = pl.DeviceIdType.MESH
NZ, NY, NX = 8, 4, 4
ROWS, WIDTH, COLS, FEATS = 128, 4096, 512, 32
SLAB = WIDTH // NZ
HEADS = COLS // HEAD_DIM
A0, A1 = 384, 512
F32, BF16 = jnp.float32, jnp.bfloat16
SENDS, ARRIVALS = 48, 78


def kernel(tokens, cot, routes, counts, widths, shard, rows_out, grad_out,
           W, tokT, dW, proj, dl, D, hot, S, R1, R3, Rf, G, DXs, DXr,
           aZs, aZr, a1, aYs, aYr, a2, aXs, aXr,
           bXs, bXr, b1, bYs, bYr, cYs, cYr, c1, cXs, cXr, Zf, Zs, Zr,
           send_sem, recv_sem):
    me, m = lax.axis_index("dp"), lax.axis_index("mp")
    x, y, z = lax.rem(me, NX), lax.rem(me // NX, NY), me // (NX * NY)

    def device(zz, yy, xx, mm):
        return ((zz * NY + yy) * NX + xx, mm)

    place = {"x": (NX, x), "y": (NY, y), "z": (NZ, z)}

    def turn(axis, by):
        n, i = place[axis]
        return lax.rem(i + (by % n), n)

    def along(axis, by):
        j = turn(axis, by)
        return {"x": device(z, y, j, m), "y": device(z, j, x, m), "z": device(j, y, x, m)}[axis]

    partner = device(z, y, x, 1 - m)
    copies, groups = [], []

    class Group:
        def __init__(self, ref):
            self.ref, self.sem, self.bytes, self.done = ref, recv_sem.at[len(groups)], 0, False
            groups.append(self)

        def send(self, src, dst, to):
            at = len(copies)
            if at >= SENDS:
                copies[at - SENDS].wait_send()
            copy = pltpu.make_async_remote_copy(
                src_ref=src, dst_ref=dst, send_sem=send_sem.at[at % SENDS], recv_sem=self.sem,
                device_id=to, device_id_type=MESH)
            copy.start()
            copies.append(copy)
            self.bytes += math.prod(src.shape) * src.dtype.itemsize

        def wait(self):
            assert self.bytes == math.prod(self.ref.shape) * self.ref.dtype.itemsize
            self.done = True
            pltpu.make_async_remote_copy(
                src_ref=self.ref, dst_ref=self.ref, send_sem=send_sem.at[0], recv_sem=self.sem,
                device_id=partner, device_id_type=MESH).wait_recv()

    barrier = pltpu.get_barrier_semaphore()
    peers = [along(axis, o) for axis in "xyz" for o in range(1, place[axis][0])] + [partner]
    for peer in peers:
        pl.semaphore_signal(barrier, inc=1, device_id=peer, device_id_type=MESH)
    W[z, y, x] = shard[...]
    pl.semaphore_wait(barrier, len(peers))

    up, down = pl.ds(0, 16), pl.ds(16, 16)
    ca, cb = pl.ds(A0, A1 - A0), pl.ds(0, A0)
    every = pl.ds(0, 4)

    def span(half):
        return every if half is None else pl.ds(half * 2, 2)

    def ring(group, axis, k, region):
        halves = (0, 1) if k == place[axis][0] // 2 else (None, None)
        right, left = region(turn(axis, 1 - k), halves[0]), region(turn(axis, k - 1), halves[1])
        group.send(right, right, along(axis, 1))
        group.send(left, left, along(axis, -1))

    class Chunk:
        def __init__(self, q):
            self.q = q

        def near(self):
            q = self.q
            self.group = Group(W.at[pl.ds(0, 6), 0, 0, up, cb])
            upper, lower = W.at[q, y, x, up, cb], W.at[q, y, x, down, cb]
            for o in range(1, 4):
                self.group.send(upper, upper, along("y", o))
                self.group.send(lower, lower, along("x", o))

        def far(self, k):
            q = self.q
            self.group.wait()
            self.group = Group(W.at[pl.ds(0, 4 // k), every, 0, up, cb])
            ring(self.group, "x", k, lambda j, h: W.at[q, span(h), j, up, cb])
            ring(self.group, "y", k, lambda j, h: W.at[q, j, span(h), down, cb])

    chunks = [Chunk(turn("z", -o)) for o in range(NZ)]
    own_bc = W.at[z, y, x, :, cb]
    from_z = {}
    for o in (4, 3, 5, 2, 6, 1, 7):
        from_z[o] = Group(W.at[0, 0, 0, :, cb])
        from_z[o].send(own_bc, own_bc, along("z", o))
    chunks[0].near()
    own_a = W.at[z, y, x, :, ca]
    a_x = Group(W.at[pl.ds(0, 3), 0, 0, :, ca])
    for o in range(1, NX):
        a_x.send(own_a, own_a, along("x", o))

    def arrive(*offsets):
        for o in offsets:
            from_z[o].wait()
            chunks[o].near()

    def far(k, *offsets):
        for o in offsets:
            chunks[o].far(k)

    a_last = {}

    def a_far(k, first, last):
        if k > 1:
            a_last[first].wait()
        a_last[first] = Group(W.at[pl.ds(0, 1 if k == 4 else 2), pl.ds(0, last - first), every, :, ca])
        for oy in range(first, last):
            row = turn("y", -oy)
            ring(a_last[first], "z", k, lambda j, h: W.at[j, row, span(h), :, ca])

    named = jnp.broadcast_to(routes[...], (ROWS, ROWS))
    first_index = lax.broadcasted_iota(jnp.int32, (ROWS, ROWS), 0)
    second_index = lax.broadcasted_iota(jnp.int32, (ROWS, ROWS), 1)
    same = (named == named.astype(F32).T.astype(jnp.int32)) & (first_index < second_index)
    earlier = jnp.sum(same.astype(F32), axis=0, keepdims=True).astype(jnp.int32)
    slot = (routes[...] * 2 + earlier) * HEADS

    def prepare(s):
        tokT[s] = tokens[:, s * SLAB:(s + 1) * SLAB].T
        for h in range(HEADS):
            hot[s, :, h * ROWS:(h + 1) * ROWS] = (first_index + s * ROWS == slot + h).astype(F32).astype(BF16)

    def forward(o):
        q = chunks[o].q
        columns = pl.ds(pl.multiple_of(q * SLAB, SLAB), SLAB)
        term = jnp.dot(tokens[:, columns], W[q].reshape(SLAB, COLS), preferred_element_type=F32)
        if o == 0:
            proj[...] = term
        else:
            proj[...] += term

    a_x.wait()
    a_y = Group(W.at[pl.ds(0, 3), 0, every, :, ca])
    own_ay = W.at[z, y, every, :, ca]
    for o in range(1, NY):
        a_y.send(own_ay, own_ay, along("y", o))
    a_far(1, 0, 1)
    far(1, 0)
    arrive(1, 7)
    arrive(2, 6)
    a_y.wait()
    a_far(1, 1, 4)
    far(1, 1, 7)
    arrive(3, 5)
    a_far(2, 0, 1)
    far(2, 0)
    arrive(4)
    far(1, 2, 6)
    prepare(0)
    a_far(2, 1, 4)
    far(2, 1, 7)
    far(1, 3, 5)
    prepare(1)
    prepare(2)
    a_far(3, 0, 1)
    far(2, 2, 6)
    far(1, 4)
    prepare(3)
    prepare(4)
    a_far(3, 1, 4)
    a_far(4, 0, 1)
    far(2, 3, 5)
    far(2, 4)
    prepare(5)
    prepare(6)
    chunks[0].group.wait()
    forward(0)
    prepare(7)
    chunks[1].group.wait()
    forward(1)
    chunks[7].group.wait()
    forward(7)
    a_far(4, 1, 4)
    for o in (2, 6, 3, 5):
        chunks[o].group.wait()
        forward(o)
    a_last[0].wait()
    a_last[1].wait()
    chunks[4].group.wait()
    forward(4)

    position = lax.broadcasted_iota(jnp.int32, (ROWS, 1), 0)
    bound0 = counts[0, 0]
    bound1 = bound0 + counts[0, 1]
    bound2 = bound1 + counts[0, 2]
    row_width = jnp.where(position < bound0, widths[0], jnp.where(
        position < bound1, widths[1], jnp.where(position < bound2, widths[2], widths[3])))
    for h in range(HEADS):
        cols = slice(h * HEAD_DIM, (h + 1) * HEAD_DIM)
        own = proj[:, cols]
        inverse = 1.0 / jnp.sqrt(jnp.mean(own * own, axis=1, keepdims=True) + EPSILON)
        outputs = own * inverse
        head_mask = (m * HEADS + h < row_width).astype(F32)
        upstream = cot[:, cols].astype(F32) * head_mask
        delta = (upstream - outputs * jnp.mean(upstream * outputs, axis=1, keepdims=True)) * inverse
        dl[:, cols] = delta.astype(BF16)
        D[h * ROWS:(h + 1) * ROWS] = delta.astype(BF16)

    def reduce(group, axis, lead, t, local, sbuf, rbuf):
        n, half = place[axis][0], lead // 2
        for d in range(2):
            by = n // 2 - t + 1
            j = turn(axis, by if d == 0 else -by)

            def put(lo, hi, arrived):
                value = local(j, lo, hi)
                if arrived:
                    value += rbuf[d, t - 2, lo:hi].astype(F32)
                sbuf[d, t - 1, lo:hi] = value.astype(BF16)

            first = d * half
            part = pl.ds(0, lead)
            if t == 1:
                put(first, first + half, False)
                part = pl.ds(first, half)
            elif t == 2:
                put(first, first + half, True)
                put(half - first, lead - first, False)
            else:
                put(0, half, True)
                put(half, lead, True)
            group.send(sbuf.at[d, t - 1, part], rbuf.at[d, t - 1, part], along(axis, 1 if d == 0 else -1))

    def ring_sum(axis, lead, local, rbuf):
        n, i = place[axis]
        s = n // 2 - 1
        return (local(i, 0, lead) + rbuf[0, s].astype(F32)) + rbuf[1, s].astype(F32)

    def a_local(j, lo, hi):
        return dW[j, lo:hi, :, :, A0:A1]

    a_group = {}

    def a_step(t):
        if t > 1:
            a_group[t - 1].wait()
        a_group[t] = Group(aZr.at[0, 0] if t == 1 else aZr.at[:, 0])
        reduce(a_group[t], "z", NY, t, a_local, aZs, aZr)

    class Unit:
        def __init__(self, at, o):
            self.at, self.o, self.q = at, o, turn("z", -o)
            q = self.q
            self.b_local = lambda j, lo, hi: dW[q, lo:hi, j, 0:16, 0:A0]
            self.c_local = lambda j, lo, hi: dW[q, j, lo:hi, 16:32, 0:A0]

        def term(self):
            part = jnp.dot(tokT[self.q], dl[...], preferred_element_type=F32)
            dW[self.q] = part.reshape(NY, NX, FEATS, COLS)

        def step(self, t):
            at = self.at
            if t > 1:
                self.group.wait()
            self.group = Group(bXr.at[at, :, 0] if t == 1 else bXr.at[at])
            reduce(self.group, "x", NY, t, self.b_local, bXs.at[at], bXr.at[at])
            reduce(self.group, "y", NX, t, self.c_local, cYs.at[at], cYr.at[at])

        def near(self):
            at = self.at
            self.group.wait()
            self.group = Group(W.at[pl.ds(0, 6), 0, 0, up, cb])
            total = ring_sum("x", NY, self.b_local, bXr.at[at])
            b1[at] = total
            bYs[at] = total.astype(BF16)
            for o in range(1, 4):
                self.group.send(bYs.at[at, turn("y", o)], bYr.at[at, o - 1], along("y", o))
            total = ring_sum("y", NX, self.c_local, cYr.at[at])
            c1[at] = total
            cXs[at] = total.astype(BF16)
            for o in range(1, 4):
                self.group.send(cXs.at[at, turn("x", o)], cXr.at[at, o - 1], along("x", o))

        def across(self):
            at = self.at
            self.group.wait()
            for mine, arrived, rows, i in ((b1, bYr, slice(0, 16), y), (c1, cXr, slice(16, 32), x)):
                total = mine[at, i]
                for k in range(3):
                    total += arrived[at, k].astype(F32)
                if self.o == 0:
                    Zf[rows] = total
                else:
                    Zs[at, rows] = total.astype(BF16)
            if self.o:
                to_z.send(Zs.at[at], Zr.at[self.o - 1], along("z", -self.o))

    to_z = Group(Zr)
    units = [Unit(at, o) for at, o in enumerate((4, 3, 5, 2, 6, 1, 7, 0))]
    for unit in units[:4]:
        unit.term()
        unit.step(1)

    r_z = Group(R1.at[pl.ds(0, 7)])
    S_order = (4, 3, 5, 2, 6, 1, 7, 0)
    for o in S_order:
        j = turn("z", o)
        packed = jnp.dot(hot[j], D[...], preferred_element_type=F32)
        packed = packed.reshape(NY, NX, 8, HEAD_DIM).astype(BF16)
        if o:
            S[j] = packed
            r_z.send(S.at[j], R1.at[z], along("z", o))
        else:
            R1[z] = packed
    for unit in units[4:]:
        unit.term()
        unit.step(1)
    a_step(1)
    for unit in units[:4]:
        unit.step(2)
    a_step(2)
    all_z = pl.ds(0, NZ)
    r_z.wait()
    r_xy = Group(W.at[pl.ds(0, 5), pl.ds(0, 3), pl.ds(0, 2), :, ca])
    for oy in range(NY):
        for ox in range(NX):
            jy, jx = turn("y", oy), turn("x", ox)
            if oy or ox:
                r_xy.send(R1.at[all_z, jy, jx], R3.at[all_z, y, x], device(z, jy, jx, m))
    for s in range(NZ):
        R3[s, y, x] = R1[s, y, x]
    units[0].near()
    units[4].step(2)
    units[1].near()
    units[5].step(2)
    a_step(3)
    units[2].near()
    units[6].step(2)
    units[0].across()
    units[3].near()
    units[7].step(2)
    units[1].across()
    units[4].near()
    units[2].across()
    a_step(4)

    r_xy.wait()
    Rf[...] = R3[...].astype(F32).reshape(8 * ROWS, HEAD_DIM)
    for h in range(HEADS):
        G[:, h * HEAD_DIM:(h + 1) * HEAD_DIM] = Rf[pl.ds(h, 2 * ROWS, stride=HEADS), :].astype(BF16)

    def product(tile):
        return lax.dot_general(G[...], W[tile].reshape(SLAB, COLS), (((1,), (1,)), ((), ())),
                               preferred_element_type=F32).astype(BF16)

    halves = []

    def give(t):
        DXs[t] = product((1 - m) * 4 + t)
        group = Group(DXr.at[t])
        group.send(DXs.at[t], DXr.at[t], partner)
        halves.append(group)

    def take(t):
        own = product(m * 4 + t).astype(F32)
        halves[t].wait()
        rows_out[:, t * SLAB:(t + 1) * SLAB] = (own + DXr[t].astype(F32)).astype(BF16)

    give(0)
    units[5].near()
    units[3].across()
    give(1)
    units[6].near()
    units[4].across()
    a_group[4].wait()
    total = ring_sum("z", NY, a_local, aZr)
    a1[...] = total
    aYs[...] = total.astype(BF16)
    ra_y = Group(aYr)
    for o in range(1, NY):
        ra_y.send(aYs.at[turn("y", o)], aYr.at[o - 1], along("y", o))
    units[7].near()
    units[5].across()
    give(2)
    units[6].across()
    give(3)
    ra_y.wait()
    total = a1[y]
    for o in range(NY - 1):
        total += aYr[o].astype(F32)
    a2[...] = total
    aXs[...] = total.astype(BF16)
    ra_x = Group(aXr)
    for o in range(1, NX):
        ra_x.send(aXs.at[turn("x", o)], aXr.at[o - 1], along("x", o))
    units[7].across()
    for t in range(4):
        take(t)
    scale = 1.0 / 128.0
    to_z.wait()
    total = Zf[...]
    for o in range(NZ - 1):
        total += Zr[o].astype(F32)
    grad_out[:, 0:A0] = total * scale
    ra_x.wait()
    total = a2[x]
    for o in range(NX - 1):
        total += aXr[o].astype(F32)
    grad_out[:, A0:A1] = total * scale
    assert len(groups) == ARRIVALS
    for copy in copies[-SENDS:]:
        copy.wait_send()


def per_device(tokens, key_cot, routes, counts, widths, key_weight):
    vmem = pl.BlockSpec(memory_space=pltpu.VMEM)
    smem = pl.BlockSpec(memory_space=pltpu.SMEM)
    buffers = [
        ((NZ, NY, NX, FEATS, COLS), BF16),
        ((NZ, SLAB, ROWS), BF16),
        ((NZ, NY, NX, FEATS, COLS), F32),
        ((ROWS, COLS), F32),
        ((ROWS, COLS), BF16),
        ((HEADS * ROWS, HEAD_DIM), BF16),
        ((NZ, ROWS, HEADS * ROWS), BF16),
        ((NZ, NY, NX, 8, HEAD_DIM), BF16),
        ((NZ, NY, NX, 8, HEAD_DIM), BF16),
        ((NZ, NY, NX, 8, HEAD_DIM), BF16),
        ((8 * ROWS, HEAD_DIM), F32),
        ((2 * ROWS, COLS), BF16),
        ((4, 2 * ROWS, SLAB), BF16),
        ((4, 2 * ROWS, SLAB), BF16),
        ((2, 4, NY, NX, FEATS, 128), BF16),
        ((2, 4, NY, NX, FEATS, 128), BF16),
        ((NY, NX, FEATS, 128), F32),
        ((NY, NX, FEATS, 128), BF16),
        ((NY - 1, NX, FEATS, 128), BF16),
        ((NX, FEATS, 128), F32),
        ((NX, FEATS, 128), BF16),
        ((NX - 1, FEATS, 128), BF16),
        ((NZ, 2, 2, NY, 16, 384), BF16),
        ((NZ, 2, 2, NY, 16, 384), BF16),
        ((NZ, NY, 16, 384), F32),
        ((NZ, NY, 16, 384), BF16),
        ((NZ, NY - 1, 16, 384), BF16),
        ((NZ, 2, 2, NX, 16, 384), BF16),
        ((NZ, 2, 2, NX, 16, 384), BF16),
        ((NZ, NX, 16, 384), F32),
        ((NZ, NX, 16, 384), BF16),
        ((NZ, NX - 1, 16, 384), BF16),
        ((FEATS, 384), F32),
        ((NZ, FEATS, 384), BF16),
        ((NZ - 1, FEATS, 384), BF16),
    ]
    return pl.pallas_call(
        kernel,
        out_shape=(jax.ShapeDtypeStruct((2 * ROWS, WIDTH // 2), BF16), jax.ShapeDtypeStruct((FEATS, COLS), F32)),
        in_specs=[vmem, vmem, vmem, smem, smem, vmem],
        out_specs=(vmem, vmem),
        scratch_shapes=[pltpu.VMEM(shape, dtype) for shape, dtype in buffers]
        + [pltpu.SemaphoreType.DMA((SENDS,)), pltpu.SemaphoreType.DMA((ARRIVALS,))],
        compiler_params=pltpu.CompilerParams(
            collective_id=0, has_side_effects=True, vmem_limit_bytes=58 << 20),
    )(tokens, key_cot, routes.reshape(1, ROWS), counts, widths, key_weight)


def solution(mesh):
    return jax.shard_map(
        per_device,
        mesh=mesh,
        in_specs=(P("dp", None), P("dp", "mp"), P("dp", None), P("dp", None), P(), P("dp", "mp")),
        out_specs=(P("dp", "mp"), P("dp", "mp")),
        check_vma=False,
    )
```

time: 83.1 us -> 77.3 us (0.930)
  Pallas kernels: 79.3 us -> 73.5 us
    pallas_call x1, Pallas kernels: 79.3 us -> 73.5 us  [per_device(): pl.pallas_call(kernel, out_shape=(jax.ShapeDtypeStruct((2 * ROWS, WIDTH /...]
where the time goes in v3:
time: 77.3 us; the launch traced here: 77.1 us
  Pallas kernels  73.5 us (95%)
  local copies, waits for them, and re-layouts  2.97 us (4%)
    pallas_call x1, Pallas kernels, per_device(): pl.pallas_call(kernel, out_shape=(jax.ShapeDtypeStruct((2 * ROWS, WIDTH /...  73.5 us
    unnamed x4, local copies, waits for them, and re-layouts  2.97 us

profile of v3, /device:TPU:2, one launch (start us, length us, event | category | flops | bytes accessed | tf_op | source)
XLA Modules:
  0.0 77.1 jit_solution(10038777919539423850)
XLA Ops:
  0.6 73.5 %shard_map.77 = (bf16[256,2048]{1,0:T(8,128)(2,1)}, f32[32,512]{1,0:T(8,128)}) custom-call(bf16[128,4096]{1,0:T(8,128)(2,1)} %tokens.1, bf16[128,512]{1,0:T(8,128)(2,1)} %cot.1, s32[1,128]{1,0:T(1,128)} %bitcast.1, s32[1,4]{1,0:T(1,128)} %counts.1, s32[4]{0:T(128)} %widths.1, bf16[32,512]{1,0:T(8,128)(2,1)} %shard.1), custom_call_target="tpu_custom_call" | custom-call | tf_op jit(solution)/shard_map/pallas_call | solution.py:473
  74.2 0.0 copy-start
  74.2 2.3 %copy.10 = bf16[256,2048]{1,0:T(8,128)(2,1)} copy(bf16[256,2048]{1,0:T(8,128)(2,1)} %get-tuple-element.4) | data formatting | bytes 2097152
  76.5 0.0 copy-done
  76.5 0.6 copy.11
Async XLA Ops:
  74.2 2.3 %copy-start = (f32[32,512]{1,0:T(8,128)S(1)}, f32[32,512]{1,0:T(8,128)}, u32[]{:S(2)}) copy-start(f32[32,512]{1,0:T(8,128)} %get-tuple-element.5) | copy-start | bytes 196612

commit v4 on v3

--- a/solution.py
+++ b/solution.py
@@ -148,64 +148,25 @@
         for h in range(HEADS):
             hot[s, :, h * ROWS:(h + 1) * ROWS] = (first_index + s * ROWS == slot + h).astype(F32).astype(BF16)
 
+    started = []
+
     def forward(o):
         q = chunks[o].q
         columns = pl.ds(pl.multiple_of(q * SLAB, SLAB), SLAB)
         term = jnp.dot(tokens[:, columns], W[q].reshape(SLAB, COLS), preferred_element_type=F32)
-        if o == 0:
+        if not started:
+            started.append(o)
             proj[...] = term
         else:
             proj[...] += term
 
-    a_x.wait()
     a_y = Group(W.at[pl.ds(0, 3), 0, every, :, ca])
-    own_ay = W.at[z, y, every, :, ca]
-    for o in range(1, NY):
-        a_y.send(own_ay, own_ay, along("y", o))
-    a_far(1, 0, 1)
-    far(1, 0)
-    arrive(1, 7)
-    arrive(2, 6)
-    a_y.wait()
-    a_far(1, 1, 4)
-    far(1, 1, 7)
-    arrive(3, 5)
-    a_far(2, 0, 1)
-    far(2, 0)
-    arrive(4)
-    far(1, 2, 6)
-    prepare(0)
-    a_far(2, 1, 4)
-    far(2, 1, 7)
-    far(1, 3, 5)
-    prepare(1)
-    prepare(2)
-    a_far(3, 0, 1)
-    far(2, 2, 6)
-    far(1, 4)
-    prepare(3)
-    prepare(4)
-    a_far(3, 1, 4)
-    a_far(4, 0, 1)
-    far(2, 3, 5)
-    far(2, 4)
-    prepare(5)
-    prepare(6)
-    chunks[0].group.wait()
-    forward(0)
-    prepare(7)
-    chunks[1].group.wait()
-    forward(1)
-    chunks[7].group.wait()
-    forward(7)
-    a_far(4, 1, 4)
-    for o in (2, 6, 3, 5):
-        chunks[o].group.wait()
-        forward(o)
-    a_last[0].wait()
-    a_last[1].wait()
-    chunks[4].group.wait()
-    forward(4)
+
+    def a_row():
+        a_x.wait()
+        own = W.at[z, y, every, :, ca]
+        for o in range(1, NY):
+            a_y.send(own, own, along("y", o))
 
     position = lax.broadcasted_iota(jnp.int32, (ROWS, 1), 0)
     bound0 = counts[0, 0]
@@ -213,16 +174,18 @@
     bound2 = bound1 + counts[0, 2]
     row_width = jnp.where(position < bound0, widths[0], jnp.where(
         position < bound1, widths[1], jnp.where(position < bound2, widths[2], widths[3])))
-    for h in range(HEADS):
-        cols = slice(h * HEAD_DIM, (h + 1) * HEAD_DIM)
-        own = proj[:, cols]
-        inverse = 1.0 / jnp.sqrt(jnp.mean(own * own, axis=1, keepdims=True) + EPSILON)
-        outputs = own * inverse
-        head_mask = (m * HEADS + h < row_width).astype(F32)
-        upstream = cot[:, cols].astype(F32) * head_mask
-        delta = (upstream - outputs * jnp.mean(upstream * outputs, axis=1, keepdims=True)) * inverse
-        dl[:, cols] = delta.astype(BF16)
-        D[h * ROWS:(h + 1) * ROWS] = delta.astype(BF16)
+
+    def norm_grads():
+        for h in range(HEADS):
+            cols = slice(h * HEAD_DIM, (h + 1) * HEAD_DIM)
+            own = proj[:, cols]
+            inverse = 1.0 / jnp.sqrt(jnp.mean(own * own, axis=1, keepdims=True) + EPSILON)
+            outputs = own * inverse
+            head_mask = (m * HEADS + h < row_width).astype(F32)
+            upstream = cot[:, cols].astype(F32) * head_mask
+            delta = (upstream - outputs * jnp.mean(upstream * outputs, axis=1, keepdims=True)) * inverse
+            dl[:, cols] = delta.astype(BF16)
+            D[h * ROWS:(h + 1) * ROWS] = delta.astype(BF16)
 
     def reduce(group, axis, lead, t, local, sbuf, rbuf):
         n, half = place[axis][0], lead // 2
@@ -315,13 +278,12 @@
 
     to_z = Group(Zr)
     units = [Unit(at, o) for at, o in enumerate((4, 3, 5, 2, 6, 1, 7, 0))]
-    for unit in units[:4]:
-        unit.term()
-        unit.step(1)
 
     r_z = Group(R1.at[pl.ds(0, 7)])
-    S_order = (4, 3, 5, 2, 6, 1, 7, 0)
-    for o in S_order:
+    r_xy = Group(W.at[pl.ds(0, 5), pl.ds(0, 3), pl.ds(0, 2), :, ca])
+    all_z = pl.ds(0, NZ)
+
+    def pack(o):
         j = turn("z", o)
         packed = jnp.dot(hot[j], D[...], preferred_element_type=F32)
         packed = packed.reshape(NY, NX, 8, HEAD_DIM).astype(BF16)
@@ -330,42 +292,22 @@
             r_z.send(S.at[j], R1.at[z], along("z", o))
         else:
             R1[z] = packed
-    for unit in units[4:]:
-        unit.term()
-        unit.step(1)
-    a_step(1)
-    for unit in units[:4]:
-        unit.step(2)
-    a_step(2)
-    all_z = pl.ds(0, NZ)
-    r_z.wait()
-    r_xy = Group(W.at[pl.ds(0, 5), pl.ds(0, 3), pl.ds(0, 2), :, ca])
-    for oy in range(NY):
-        for ox in range(NX):
-            jy, jx = turn("y", oy), turn("x", ox)
-            if oy or ox:
-                r_xy.send(R1.at[all_z, jy, jx], R3.at[all_z, y, x], device(z, jy, jx, m))
-    for s in range(NZ):
-        R3[s, y, x] = R1[s, y, x]
-    units[0].near()
-    units[4].step(2)
-    units[1].near()
-    units[5].step(2)
-    a_step(3)
-    units[2].near()
-    units[6].step(2)
-    units[0].across()
-    units[3].near()
-    units[7].step(2)
-    units[1].across()
-    units[4].near()
-    units[2].across()
-    a_step(4)
-
-    r_xy.wait()
-    Rf[...] = R3[...].astype(F32).reshape(8 * ROWS, HEAD_DIM)
-    for h in range(HEADS):
-        G[:, h * HEAD_DIM:(h + 1) * HEAD_DIM] = Rf[pl.ds(h, 2 * ROWS, stride=HEADS), :].astype(BF16)
+
+    def route_plane():
+        r_z.wait()
+        for oy in range(NY):
+            for ox in range(NX):
+                jy, jx = turn("y", oy), turn("x", ox)
+                if oy or ox:
+                    r_xy.send(R1.at[all_z, jy, jx], R3.at[all_z, y, x], device(z, jy, jx, m))
+        for s in range(NZ):
+            R3[s, y, x] = R1[s, y, x]
+
+    def unpack():
+        r_xy.wait()
+        Rf[...] = R3[...].astype(F32).reshape(8 * ROWS, HEAD_DIM)
+        for h in range(HEADS):
+            G[:, h * HEAD_DIM:(h + 1) * HEAD_DIM] = Rf[pl.ds(h, 2 * ROWS, stride=HEADS), :].astype(BF16)
 
     def product(tile):
         return lax.dot_general(G[...], W[tile].reshape(SLAB, COLS), (((1,), (1,)), ((), ())),
@@ -384,47 +326,167 @@
         halves[t].wait()
         rows_out[:, t * SLAB:(t + 1) * SLAB] = (own + DXr[t].astype(F32)).astype(BF16)
 
+    ra_y, ra_x = Group(aYr), Group(aXr)
+    scale = 1.0 / 128.0
+
+    def a_over_y():
+        a_group[4].wait()
+        total = ring_sum("z", NY, a_local, aZr)
+        a1[...] = total
+        aYs[...] = total.astype(BF16)
+        for o in range(1, NY):
+            ra_y.send(aYs.at[turn("y", o)], aYr.at[o - 1], along("y", o))
+
+    def a_over_x():
+        ra_y.wait()
+        total = a1[y]
+        for o in range(NY - 1):
+            total += aYr[o].astype(F32)
+        a2[...] = total
+        aXs[...] = total.astype(BF16)
+        for o in range(1, NX):
+            ra_x.send(aXs.at[turn("x", o)], aXr.at[o - 1], along("x", o))
+
+    def finish_bc():
+        to_z.wait()
+        total = Zf[...]
+        for o in range(NZ - 1):
+            total += Zr[o].astype(F32)
+        grad_out[:, 0:A0] = total * scale
+
+    def finish_a():
+        ra_x.wait()
+        total = a2[x]
+        for o in range(NX - 1):
+            total += aXr[o].astype(F32)
+        grad_out[:, A0:A1] = total * scale
+
+    prepare(4)
+    a_row()
+    chunks[0].far(1)
+    a_far(1, 0, 1)
+    prepare(0)
+    arrive(4)
+    arrive(6)
+    arrive(7)
+    arrive(1)
+    a_far(2, 0, 1)
+    arrive(3)
+    a_y.wait()
+    a_far(1, 1, 4)
+    arrive(2)
+    prepare(6)
+    chunks[0].far(2)
+    arrive(5)
+    a_far(3, 0, 1)
+    chunks[4].far(1)
+    prepare(1)
+    chunks[6].far(1)
+    chunks[3].far(1)
+    a_far(2, 1, 4)
+    prepare(7)
+    chunks[2].far(1)
+    prepare(5)
+    chunks[1].far(1)
+    chunks[7].far(1)
+    chunks[5].far(1)
+    chunks[3].far(2)
+    a_far(3, 1, 4)
+    a_far(4, 0, 1)
+    chunks[2].far(2)
+    prepare(3)
+    chunks[1].far(2)
+    chunks[6].far(2)
+    chunks[0].group.wait()
+    forward(0)
+    chunks[4].far(2)
+    chunks[5].far(2)
+    chunks[7].far(2)
+    a_far(4, 1, 4)
+    chunks[4].group.wait()
+    chunks[6].group.wait()
+    forward(6)
+    chunks[3].group.wait()
+    forward(3)
+    chunks[5].group.wait()
+    forward(5)
+    chunks[1].group.wait()
+    forward(1)
+    chunks[2].group.wait()
+    forward(2)
+    prepare(2)
+    chunks[7].group.wait()
+    forward(7)
+    a_last[0].wait()
+    a_last[1].wait()
+    forward(4)
+    norm_grads()
+    pack(4)
+    units[4].term()
+    units[2].term()
+    units[1].term()
+    units[3].term()
+    units[0].term()
+    units[5].term()
+    units[7].term()
+    units[6].term()
+    a_step(1)
+    units[1].step(1)
+    units[4].step(1)
+    units[3].step(1)
+    pack(5)
+    pack(3)
+    units[6].step(1)
+    units[7].step(1)
+    pack(0)
+    units[0].step(1)
+    units[1].step(2)
+    a_step(2)
+    pack(6)
+    units[2].step(1)
+    units[5].step(1)
+    units[4].step(2)
+    pack(2)
+    units[6].step(2)
+    units[1].near()
+    pack(1)
+    units[3].step(2)
+    pack(7)
+    units[2].step(2)
+    a_step(3)
+    units[5].step(2)
+    units[0].step(2)
+    units[4].near()
+    route_plane()
+    a_step(4)
+    units[2].near()
+    units[5].near()
+    units[3].near()
+    units[0].near()
+    units[1].across()
+    units[7].step(2)
+    units[6].near()
+    a_over_y()
+    units[2].across()
+    unpack()
     give(0)
-    units[5].near()
+    units[0].across()
+    units[5].across()
+    units[4].across()
+    give(1)
+    give(2)
     units[3].across()
-    give(1)
-    units[6].near()
-    units[4].across()
-    a_group[4].wait()
-    total = ring_sum("z", NY, a_local, aZr)
-    a1[...] = total
-    aYs[...] = total.astype(BF16)
-    ra_y = Group(aYr)
-    for o in range(1, NY):
-        ra_y.send(aYs.at[turn("y", o)], aYr.at[o - 1], along("y", o))
     units[7].near()
-    units[5].across()
-    give(2)
+    give(3)
     units[6].across()
-    give(3)
-    ra_y.wait()
-    total = a1[y]
-    for o in range(NY - 1):
-        total += aYr[o].astype(F32)
-    a2[...] = total
-    aXs[...] = total.astype(BF16)
-    ra_x = Group(aXr)
-    for o in range(1, NX):
-        ra_x.send(aXs.at[turn("x", o)], aXr.at[o - 1], along("x", o))
+    a_over_x()
+    take(0)
+    take(1)
+    take(2)
+    take(3)
     units[7].across()
-    for t in range(4):
-        take(t)
-    scale = 1.0 / 128.0
-    to_z.wait()
-    total = Zf[...]
-    for o in range(NZ - 1):
-        total += Zr[o].astype(F32)
-    grad_out[:, 0:A0] = total * scale
-    ra_x.wait()
-    total = a2[x]
-    for o in range(NX - 1):
-        total += aXr[o].astype(F32)
-    grad_out[:, A0:A1] = total * scale
+    finish_bc()
+    finish_a()
     assert len(groups) == ARRIVALS
     for copy in copies[-SENDS:]:
         copy.wait_send()

time: 77.3 us -> 74.7 us (0.966)
  Pallas kernels: 73.5 us -> 71 us
    pallas_call x1, Pallas kernels: 73.5 us -> 71 us  [per_device(): pl.pallas_call(kernel, out_shape=(jax.ShapeDtypeStruct((2 * ROWS, WIDTH /...]
where the time goes in v4:
time: 74.7 us; the launch traced here: 74.6 us
  Pallas kernels  71 us (95%)
  local copies, waits for them, and re-layouts  2.97 us (4%)
    pallas_call x1, Pallas kernels, per_device(): pl.pallas_call(kernel, out_shape=(jax.ShapeDtypeStruct((2 * ROWS, WIDTH /...  71 us
    unnamed x4, local copies, waits for them, and re-layouts  2.97 us

profile of v4, /device:TPU:2, one launch (start us, length us, event | category | flops | bytes accessed | tf_op | source)
XLA Modules:
  0.0 74.6 jit_solution(4281627896109024496)
XLA Ops:
  0.6 71.0 %shard_map.77 = (bf16[256,2048]{1,0:T(8,128)(2,1)}, f32[32,512]{1,0:T(8,128)}) custom-call(bf16[128,4096]{1,0:T(8,128)(2,1)} %tokens.1, bf16[128,512]{1,0:T(8,128)(2,1)} %cot.1, s32[1,128]{1,0:T(1,128)} %bitcast.1, s32[1,4]{1,0:T(1,128)} %counts.1, s32[4]{0:T(128)} %widths.1, bf16[32,512]{1,0:T(8,128)(2,1)} %shard.1), custom_call_target="tpu_custom_call" | custom-call | tf_op jit(solution)/shard_map/pallas_call | solution.py:535
  71.6 0.0 copy-start
  71.6 2.3 %copy.10 = bf16[256,2048]{1,0:T(8,128)(2,1)} copy(bf16[256,2048]{1,0:T(8,128)(2,1)} %get-tuple-element.4) | data formatting | bytes 2097152
  74.0 0.0 copy-done
  74.0 0.6 copy.11
Async XLA Ops:
  71.6 2.3 %copy-start = (f32[32,512]{1,0:T(8,128)S(1)}, f32[32,512]{1,0:T(8,128)}, u32[]{:S(2)}) copy-start(f32[32,512]{1,0:T(8,128)} %get-tuple-element.5) | copy-start | bytes 196612

commit v5 on v4

--- a/solution.py
+++ b/solution.py
@@ -19,11 +19,11 @@
 SENDS, ARRIVALS = 48, 78
 
 
-def kernel(tokens, cot, routes, counts, widths, shard, rows_out, grad_out,
-           W, tokT, dW, proj, dl, D, hot, S, R1, R3, Rf, G, DXs, DXr,
+def kernel(tokens_in, cot, routes, counts, widths, shard, rows_out, grad_out,
+           tokens, rows, W, tokT, dW, proj, dl, D, hot, S, R1, R3, Rf, G, DXs, DXr,
            aZs, aZr, a1, aYs, aYr, a2, aXs, aXr,
            bXs, bXr, b1, bYs, bYr, cYs, cYr, c1, cXs, cXr, Zf, Zs, Zr,
-           send_sem, recv_sem):
+           local_sem, send_sem, recv_sem):
     me, m = lax.axis_index("dp"), lax.axis_index("mp")
     x, y, z = lax.rem(me, NX), lax.rem(me // NX, NY), me // (NX * NY)
 
@@ -65,6 +65,9 @@
             pltpu.make_async_remote_copy(
                 src_ref=self.ref, dst_ref=self.ref, send_sem=send_sem.at[0], recv_sem=self.sem,
                 device_id=partner, device_id_type=MESH).wait_recv()
+
+    fetch = pltpu.make_async_copy(tokens_in, tokens, local_sem.at[0])
+    fetch.start()
 
     barrier = pltpu.get_barrier_semaphore()
     peers = [along(axis, o) for axis in "xyz" for o in range(1, place[axis][0])] + [partner]
@@ -313,7 +316,7 @@
         return lax.dot_general(G[...], W[tile].reshape(SLAB, COLS), (((1,), (1,)), ((), ())),
                                preferred_element_type=F32).astype(BF16)
 
-    halves = []
+    halves, stores = [], []
 
     def give(t):
         DXs[t] = product((1 - m) * 4 + t)
@@ -324,7 +327,10 @@
     def take(t):
         own = product(m * 4 + t).astype(F32)
         halves[t].wait()
-        rows_out[:, t * SLAB:(t + 1) * SLAB] = (own + DXr[t].astype(F32)).astype(BF16)
+        columns = pl.ds(t * SLAB, SLAB)
+        rows[:, t * SLAB:(t + 1) * SLAB] = (own + DXr[t].astype(F32)).astype(BF16)
+        stores.append(pltpu.make_async_copy(rows.at[:, columns], rows_out.at[:, columns], local_sem.at[1 + t]))
+        stores[-1].start()
 
     ra_y, ra_x = Group(aYr), Group(aXr)
     scale = 1.0 / 128.0
@@ -361,6 +367,7 @@
             total += aXr[o].astype(F32)
         grad_out[:, A0:A1] = total * scale
 
+    fetch.wait()
     prepare(4)
     a_row()
     chunks[0].far(1)
@@ -490,12 +497,32 @@
     assert len(groups) == ARRIVALS
     for copy in copies[-SENDS:]:
         copy.wait_send()
+    for store in stores:
+        store.wait()
+
+
+PIECES = 8
+
+
+def hand_on(rows, grad, rows_out, grad_out, sem):
+    copies = [pltpu.make_async_copy(grad, grad_out, sem.at[PIECES])]
+    size = rows.shape[0] // PIECES
+    for i in range(PIECES):
+        part = pl.ds(i * size, size)
+        copies.append(pltpu.make_async_copy(rows.at[part], rows_out.at[part], sem.at[i]))
+    for copy in copies:
+        copy.start()
+    for copy in copies:
+        copy.wait()
 
 
 def per_device(tokens, key_cot, routes, counts, widths, key_weight):
     vmem = pl.BlockSpec(memory_space=pltpu.VMEM)
     smem = pl.BlockSpec(memory_space=pltpu.SMEM)
+    anywhere = pl.BlockSpec(memory_space=pl.ANY)
     buffers = [
+        ((ROWS, WIDTH), BF16),
+        ((2 * ROWS, WIDTH // 2), BF16),
         ((NZ, NY, NX, FEATS, COLS), BF16),
         ((NZ, SLAB, ROWS), BF16),
         ((NZ, NY, NX, FEATS, COLS), F32),
@@ -532,16 +559,23 @@
         ((NZ, FEATS, 384), BF16),
         ((NZ - 1, FEATS, 384), BF16),
     ]
-    return pl.pallas_call(
+    rows, grad = pl.pallas_call(
         kernel,
         out_shape=(jax.ShapeDtypeStruct((2 * ROWS, WIDTH // 2), BF16), jax.ShapeDtypeStruct((FEATS, COLS), F32)),
-        in_specs=[vmem, vmem, vmem, smem, smem, vmem],
-        out_specs=(vmem, vmem),
+        in_specs=[anywhere, vmem, vmem, smem, smem, vmem],
+        out_specs=(anywhere, vmem),
         scratch_shapes=[pltpu.VMEM(shape, dtype) for shape, dtype in buffers]
-        + [pltpu.SemaphoreType.DMA((SENDS,)), pltpu.SemaphoreType.DMA((ARRIVALS,))],
+        + [pltpu.SemaphoreType.DMA((5,)), pltpu.SemaphoreType.DMA((SENDS,)), pltpu.SemaphoreType.DMA((ARRIVALS,))],
         compiler_params=pltpu.CompilerParams(
             collective_id=0, has_side_effects=True, vmem_limit_bytes=58 << 20),
     )(tokens, key_cot, routes.reshape(1, ROWS), counts, widths, key_weight)
+    return pl.pallas_call(
+        hand_on,
+        out_shape=(jax.ShapeDtypeStruct(rows.shape, BF16), jax.ShapeDtypeStruct(grad.shape, F32)),
+        in_specs=[anywhere, anywhere],
+        out_specs=(anywhere, anywhere),
+        scratch_shapes=[pltpu.SemaphoreType.DMA((PIECES + 1,))],
+    )(rows, grad)
 
 
 def solution(mesh):

time: 74.7 us -> 106 us (1.42)
  Pallas kernels: 71 us -> 105 us
  local copies, waits for them, and re-layouts: 2.97 us -> 0 us
    pallas_call x0 -> x1, Pallas kernels: none -> 34.9 us  [per_device(): pl.pallas_call(hand_on, out_shape=(jax.ShapeDtypeStruct(rows.shape, BF16)...]
    unnamed x4 -> x0, local copies, waits for them, and re-layouts: 2.97 us -> none
where the time goes in v5:
time: 106 us
  Pallas kernels  105 us (99%)
    pallas_call x1, Pallas kernels, per_device(): pl.pallas_call(kernel, out_shape=(jax.ShapeDtypeStruct((2 * ROWS, WIDTH /...  70.3 us
    pallas_call x1, Pallas kernels, per_device(): pl.pallas_call(hand_on, out_shape=(jax.ShapeDtypeStruct(rows.shape, BF16)...  34.9 us

profile of v5, /device:TPU:2, one launch (start us, length us, event | category | flops | bytes accessed | tf_op | source)
XLA Modules:
  0.0 105.9 jit_solution(11101136409881544081)
XLA Ops:
  0.6 70.3 %shard_map.77 = (bf16[256,2048]{1,0:T(8,128)(2,1)}, f32[32,512]{1,0:T(8,128)}) custom-call(bf16[128,4096]{1,0:T(8,128)(2,1)} %tokens_in.1, bf16[128,512]{1,0:T(8,128)(2,1)} %cot.1, s32[1,128]{1,0:T(1,128)} %bitcast.1, s32[1,4]{1,0:T(1,128)} %counts.1, s32[4]{0:T(128)} %widths.1, bf16[32,512]{1,0:T(8,128)(2,1)} %shard.1), custom_call_target="tpu_custom_call" | custom-call | tf_op jit(solution)/shard_map/pallas_call | solution.py:562
  70.9 34.9 %shard_map.78 = (bf16[256,2048]{1,0:T(8,128)(2,1)}, f32[32,512]{1,0:T(8,128)}) custom-call(bf16[256,2048]{1,0:T(8,128)(2,1)} %get-tuple-element.4.rows, f32[32,512]{1,0:T(8,128)} %get-tuple-element.5.grad), custom_call_target="tpu_custom_call" | custom-call | tf_op jit(solution)/shard_map/pallas_call | solution.py:572

commit v6 on v4

--- a/solution.py
+++ b/solution.py
@@ -19,11 +19,11 @@
 SENDS, ARRIVALS = 48, 78
 
 
-def kernel(tokens, cot, routes, counts, widths, shard, rows_out, grad_out,
-           W, tokT, dW, proj, dl, D, hot, S, R1, R3, Rf, G, DXs, DXr,
+def kernel(tokens_in, cot, routes, counts, widths, shard, rows_out, grad_out,
+           tokens, W, tokT, dW, proj, dl, D, hot, S, R1, R3, Rf, G, DXs, DXr,
            aZs, aZr, a1, aYs, aYr, a2, aXs, aXr,
            bXs, bXr, b1, bYs, bYr, cYs, cYr, c1, cXs, cXr, Zf, Zs, Zr,
-           send_sem, recv_sem):
+           local_sem, send_sem, recv_sem):
     me, m = lax.axis_index("dp"), lax.axis_index("mp")
     x, y, z = lax.rem(me, NX), lax.rem(me // NX, NY), me // (NX * NY)
 
@@ -65,6 +65,9 @@
             pltpu.make_async_remote_copy(
                 src_ref=self.ref, dst_ref=self.ref, send_sem=send_sem.at[0], recv_sem=self.sem,
                 device_id=partner, device_id_type=MESH).wait_recv()
+
+    fetch = pltpu.make_async_copy(tokens_in, tokens, local_sem.at[0])
+    fetch.start()
 
     barrier = pltpu.get_barrier_semaphore()
     peers = [along(axis, o) for axis in "xyz" for o in range(1, place[axis][0])] + [partner]
@@ -361,6 +364,7 @@
             total += aXr[o].astype(F32)
         grad_out[:, A0:A1] = total * scale
 
+    fetch.wait()
     prepare(4)
     a_row()
     chunks[0].far(1)
@@ -495,7 +499,9 @@
 def per_device(tokens, key_cot, routes, counts, widths, key_weight):
     vmem = pl.BlockSpec(memory_space=pltpu.VMEM)
     smem = pl.BlockSpec(memory_space=pltpu.SMEM)
+    anywhere = pl.BlockSpec(memory_space=pl.ANY)
     buffers = [
+        ((ROWS, WIDTH), BF16),
         ((NZ, NY, NX, FEATS, COLS), BF16),
         ((NZ, SLAB, ROWS), BF16),
         ((NZ, NY, NX, FEATS, COLS), F32),
@@ -532,16 +538,17 @@
         ((NZ, FEATS, 384), BF16),
         ((NZ - 1, FEATS, 384), BF16),
     ]
-    return pl.pallas_call(
+    rows, grad = pl.pallas_call(
         kernel,
-        out_shape=(jax.ShapeDtypeStruct((2 * ROWS, WIDTH // 2), BF16), jax.ShapeDtypeStruct((FEATS, COLS), F32)),
-        in_specs=[vmem, vmem, vmem, smem, smem, vmem],
+        out_shape=(pltpu.VMEM((2 * ROWS, WIDTH // 2), BF16), pltpu.VMEM((FEATS, COLS), F32)),
+        in_specs=[anywhere, vmem, vmem, smem, smem, vmem],
         out_specs=(vmem, vmem),
         scratch_shapes=[pltpu.VMEM(shape, dtype) for shape, dtype in buffers]
-        + [pltpu.SemaphoreType.DMA((SENDS,)), pltpu.SemaphoreType.DMA((ARRIVALS,))],
+        + [pltpu.SemaphoreType.DMA((1,)), pltpu.SemaphoreType.DMA((SENDS,)), pltpu.SemaphoreType.DMA((ARRIVALS,))],
         compiler_params=pltpu.CompilerParams(
             collective_id=0, has_side_effects=True, vmem_limit_bytes=58 << 20),
     )(tokens, key_cot, routes.reshape(1, ROWS), counts, widths, key_weight)
+    return rows, grad
 
 
 def solution(mesh):

time: 74.7 us -> 72 us (0.964)
  Pallas kernels: 71 us -> 69.6 us
  local copies, waits for them, and re-layouts: 2.97 us -> 1.6 us
    unnamed x4 -> x2, local copies, waits for them, and re-layouts: 2.97 us -> 1.6 us
    pallas_call x1, Pallas kernels: 71 us -> 69.6 us  [per_device(): pl.pallas_call(kernel, out_shape=(pltpu.VMEM((2 * ROWS, WIDTH // 2), BF16...]
where the time goes in v6:
time: 72 us; the launch traced here: 71.9 us
  Pallas kernels  69.6 us (97%)
  local copies, waits for them, and re-layouts  1.6 us (2%)
    pallas_call x1, Pallas kernels, per_device(): pl.pallas_call(kernel, out_shape=(pltpu.VMEM((2 * ROWS, WIDTH // 2), BF16...  69.6 us
    unnamed x2, local copies, waits for them, and re-layouts  1.6 us

profile of v6, /device:TPU:2, one launch (start us, length us, event | category | flops | bytes accessed | tf_op | source)
XLA Modules:
  0.0 71.9 jit_solution(4320024492619364475)
XLA Ops:
  0.6 69.6 %shard_map.77 = (bf16[256,2048]{1,0:T(8,128)(2,1)S(1)}, f32[32,512]{1,0:T(8,128)S(1)}) custom-call(bf16[128,4096]{1,0:T(8,128)(2,1)} %tokens_in.1, bf16[128,512]{1,0:T(8,128)(2,1)} %cot.1, s32[1,128]{1,0:T(1,128)} %bitcast.1, s32[1,4]{1,0:T(1,128)} %counts.1, s32[4]{0:T(128)} %widths.1, bf16[32,512]{1,0:T(8,128)(2,1)} %shard.1), custom_call_target="tpu_custom_call" | custom-call | tf_op jit(solution)/shard_map/pallas_call | solution.py:541
  70.3 1.0 %copy.10 = bf16[256,2048]{1,0:T(8,128)(2,1)} copy(bf16[256,2048]{1,0:T(8,128)(2,1)S(1)} %get-tuple-element.2) | data formatting | bytes 2097152
  71.2 0.6 copy.11

commit v7 on v6

--- a/solution.py
+++ b/solution.py
@@ -16,7 +16,7 @@
 HEADS = COLS // HEAD_DIM
 A0, A1 = 384, 512
 F32, BF16 = jnp.float32, jnp.bfloat16
-SENDS, ARRIVALS = 48, 78
+SENDS, ARRIVALS = 48, 98
 
 
 def kernel(tokens_in, cot, routes, counts, widths, shard, rows_out, grad_out,
@@ -131,13 +131,12 @@
 
     a_last = {}
 
-    def a_far(k, first, last):
+    def a_far(k, oy):
         if k > 1:
-            a_last[first].wait()
-        a_last[first] = Group(W.at[pl.ds(0, 1 if k == 4 else 2), pl.ds(0, last - first), every, :, ca])
-        for oy in range(first, last):
-            row = turn("y", -oy)
-            ring(a_last[first], "z", k, lambda j, h: W.at[j, row, span(h), :, ca])
+            a_last[oy].wait()
+        a_last[oy] = Group(W.at[0, 0, every, :, ca] if k == 4 else W.at[pl.ds(0, 2), 0, every, :, ca])
+        row = turn("y", -oy)
+        ring(a_last[oy], "z", k, lambda j, h: W.at[j, row, span(h), :, ca])
 
     named = jnp.broadcast_to(routes[...], (ROWS, ROWS))
     first_index = lax.broadcasted_iota(jnp.int32, (ROWS, ROWS), 0)
@@ -220,16 +219,17 @@
         s = n // 2 - 1
         return (local(i, 0, lead) + rbuf[0, s].astype(F32)) + rbuf[1, s].astype(F32)
 
-    def a_local(j, lo, hi):
-        return dW[j, lo:hi, :, :, A0:A1]
+    def a_local(k):
+        row = turn("y", k)
+        return lambda j, lo, hi: dW[j, row, lo:hi, :, A0:A1]
 
     a_group = {}
 
-    def a_step(t):
+    def a_step(t, k):
         if t > 1:
-            a_group[t - 1].wait()
-        a_group[t] = Group(aZr.at[0, 0] if t == 1 else aZr.at[:, 0])
-        reduce(a_group[t], "z", NY, t, a_local, aZs, aZr)
+            a_group[k].wait()
+        a_group[k] = Group(aZr.at[k, 0, 0] if t == 1 else aZr.at[k, :, 0])
+        reduce(a_group[k], "z", NX, t, a_local(k), aZs.at[k], aZr.at[k])
 
     class Unit:
         def __init__(self, at, o):
@@ -332,17 +332,18 @@
     ra_y, ra_x = Group(aYr), Group(aXr)
     scale = 1.0 / 128.0
 
-    def a_over_y():
-        a_group[4].wait()
-        total = ring_sum("z", NY, a_local, aZr)
-        a1[...] = total
-        aYs[...] = total.astype(BF16)
-        for o in range(1, NY):
-            ra_y.send(aYs.at[turn("y", o)], aYr.at[o - 1], along("y", o))
+    def a_over_y(k):
+        a_group[k].wait()
+        total = ring_sum("z", NX, a_local(k), aZr.at[k])
+        if k == 0:
+            a1[...] = total
+        else:
+            aYs[k - 1] = total.astype(BF16)
+            ra_y.send(aYs.at[k - 1], aYr.at[k - 1], along("y", k))
 
     def a_over_x():
         ra_y.wait()
-        total = a1[y]
+        total = a1[...]
         for o in range(NY - 1):
             total += aYr[o].astype(F32)
         a2[...] = total
@@ -365,130 +366,155 @@
         grad_out[:, A0:A1] = total * scale
 
     fetch.wait()
+    a_row()
+    a_far(1, 0)
+    prepare(1)
+    arrive(4)
+    chunks[0].far(1)
     prepare(4)
-    a_row()
-    chunks[0].far(1)
-    a_far(1, 0, 1)
+    arrive(5)
+    arrive(3)
+    arrive(2)
+    arrive(1)
+    a_far(2, 0)
+    arrive(6)
+    a_y.wait()
+    a_far(1, 1)
+    a_far(1, 2)
+    a_far(1, 3)
+    prepare(5)
+    arrive(7)
+    chunks[0].far(2)
+    chunks[4].far(1)
+    chunks[3].far(1)
+    prepare(6)
+    a_far(3, 0)
+    a_far(2, 1)
+    chunks[2].far(1)
+    prepare(3)
+    a_far(2, 2)
+    chunks[7].far(1)
+    a_far(2, 3)
+    chunks[1].far(1)
+    a_far(4, 0)
+    chunks[6].far(1)
+    a_far(3, 1)
+    chunks[5].far(1)
+    a_far(3, 2)
     prepare(0)
-    arrive(4)
-    arrive(6)
-    arrive(7)
-    arrive(1)
-    a_far(2, 0, 1)
-    arrive(3)
-    a_y.wait()
-    a_far(1, 1, 4)
-    arrive(2)
-    prepare(6)
-    chunks[0].far(2)
-    arrive(5)
-    a_far(3, 0, 1)
-    chunks[4].far(1)
-    prepare(1)
-    chunks[6].far(1)
-    chunks[3].far(1)
-    a_far(2, 1, 4)
-    prepare(7)
-    chunks[2].far(1)
-    prepare(5)
-    chunks[1].far(1)
-    chunks[7].far(1)
-    chunks[5].far(1)
-    chunks[3].far(2)
-    a_far(3, 1, 4)
-    a_far(4, 0, 1)
-    chunks[2].far(2)
-    prepare(3)
-    chunks[1].far(2)
-    chunks[6].far(2)
+    a_far(3, 3)
     chunks[0].group.wait()
     forward(0)
     chunks[4].far(2)
+    chunks[7].far(2)
+    chunks[3].far(2)
+    chunks[1].far(2)
+    a_far(4, 1)
+    chunks[2].far(2)
+    chunks[6].far(2)
+    a_far(4, 2)
     chunks[5].far(2)
-    chunks[7].far(2)
-    a_far(4, 1, 4)
+    a_far(4, 3)
     chunks[4].group.wait()
+    chunks[3].group.wait()
+    forward(3)
+    prepare(7)
+    chunks[2].group.wait()
+    forward(2)
+    chunks[7].group.wait()
+    forward(7)
+    chunks[1].group.wait()
+    forward(1)
+    prepare(2)
     chunks[6].group.wait()
     forward(6)
-    chunks[3].group.wait()
-    forward(3)
+    a_last[0].wait()
+    a_last[1].wait()
+    a_last[2].wait()
+    a_last[3].wait()
+    forward(4)
     chunks[5].group.wait()
     forward(5)
-    chunks[1].group.wait()
-    forward(1)
-    chunks[2].group.wait()
-    forward(2)
-    prepare(2)
-    chunks[7].group.wait()
-    forward(7)
-    a_last[0].wait()
-    a_last[1].wait()
-    forward(4)
     norm_grads()
+    units[6].term()
     pack(4)
+    units[6].step(1)
+    units[5].term()
+    units[5].step(1)
+    units[0].term()
+    units[0].step(1)
+    a_step(1, 2)
+    a_step(1, 3)
     units[4].term()
+    units[4].step(1)
+    units[1].term()
+    a_step(1, 1)
+    units[1].step(1)
+    pack(5)
+    units[3].term()
+    units[3].step(1)
+    pack(3)
     units[2].term()
-    units[1].term()
-    units[3].term()
-    units[0].term()
-    units[5].term()
+    units[2].step(1)
     units[7].term()
-    units[6].term()
-    a_step(1)
-    units[1].step(1)
-    units[4].step(1)
-    units[3].step(1)
-    pack(5)
-    pack(3)
-    units[6].step(1)
     units[7].step(1)
+    units[6].step(2)
+    a_step(1, 0)
+    pack(7)
+    a_step(2, 2)
+    units[0].step(2)
+    a_step(2, 1)
+    units[4].step(2)
+    a_step(2, 3)
+    pack(6)
+    pack(2)
+    units[2].step(2)
+    units[1].step(2)
+    pack(1)
+    units[5].step(2)
+    units[6].near()
+    a_step(2, 0)
+    a_step(3, 2)
+    units[0].near()
+    units[3].step(2)
+    units[4].near()
+    a_step(3, 1)
+    a_step(3, 3)
     pack(0)
-    units[0].step(1)
-    units[1].step(2)
-    a_step(2)
-    pack(6)
-    units[2].step(1)
-    units[5].step(1)
-    units[4].step(2)
-    pack(2)
-    units[6].step(2)
+    route_plane()
     units[1].near()
-    pack(1)
-    units[3].step(2)
-    pack(7)
-    units[2].step(2)
-    a_step(3)
-    units[5].step(2)
-    units[0].step(2)
-    units[4].near()
-    route_plane()
-    a_step(4)
+    a_step(3, 0)
     units[2].near()
+    a_step(4, 2)
+    a_step(4, 1)
     units[5].near()
+    a_step(4, 3)
     units[3].near()
-    units[0].near()
+    units[7].step(2)
+    a_step(4, 0)
+    units[4].across()
+    a_over_y(2)
+    a_over_y(1)
+    a_over_y(3)
+    units[0].across()
     units[1].across()
-    units[7].step(2)
-    units[6].near()
-    a_over_y()
+    unpack()
     units[2].across()
-    unpack()
     give(0)
-    units[0].across()
-    units[5].across()
-    units[4].across()
     give(1)
     give(2)
+    give(3)
     units[3].across()
     units[7].near()
-    give(3)
+    units[5].across()
     units[6].across()
+    a_over_y(0)
     a_over_x()
     take(0)
     take(1)
     take(2)
+    units[7].across()
     take(3)
-    units[7].across()
     finish_bc()
     finish_a()
     assert len(groups) == ARRIVALS
@@ -516,10 +542,10 @@
         ((2 * ROWS, COLS), BF16),
         ((4, 2 * ROWS, SLAB), BF16),
         ((4, 2 * ROWS, SLAB), BF16),
-        ((2, 4, NY, NX, FEATS, 128), BF16),
-        ((2, 4, NY, NX, FEATS, 128), BF16),
-        ((NY, NX, FEATS, 128), F32),
-        ((NY, NX, FEATS, 128), BF16),
+        ((NY, 2, 4, NX, FEATS, 128), BF16),
+        ((NY, 2, 4, NX, FEATS, 128), BF16),
+        ((NX, FEATS, 128), F32),
+        ((NY - 1, NX, FEATS, 128), BF16),
         ((NY - 1, NX, FEATS, 128), BF16),
         ((NX, FEATS, 128), F32),
         ((NX, FEATS, 128), BF16),

time: 72 us -> 65.1 us (0.904)
  Pallas kernels: 69.6 us -> 62.8 us
    pallas_call x1, Pallas kernels: 69.6 us -> 62.8 us  [per_device(): pl.pallas_call(kernel, out_shape=(pltpu.VMEM((2 * ROWS, WIDTH // 2), BF16...]
where the time goes in v7:
time: 65.1 us; the launch traced here: 65 us
  Pallas kernels  62.8 us (96%)
  local copies, waits for them, and re-layouts  1.6 us (2%)
    pallas_call x1, Pallas kernels, per_device(): pl.pallas_call(kernel, out_shape=(pltpu.VMEM((2 * ROWS, WIDTH // 2), BF16...  62.8 us
    unnamed x2, local copies, waits for them, and re-layouts  1.6 us

profile of v7, /device:TPU:2, one launch (start us, length us, event | category | flops | bytes accessed | tf_op | source)
XLA Modules:
  0.0 65.0 jit_solution(3504257017383719883)
XLA Ops:
  0.6 62.8 %shard_map.77 = (bf16[256,2048]{1,0:T(8,128)(2,1)S(1)}, f32[32,512]{1,0:T(8,128)S(1)}) custom-call(bf16[128,4096]{1,0:T(8,128)(2,1)} %tokens_in.1, bf16[128,512]{1,0:T(8,128)(2,1)} %cot.1, s32[1,128]{1,0:T(1,128)} %bitcast.1, s32[1,4]{1,0:T(1,128)} %counts.1, s32[4]{0:T(128)} %widths.1, bf16[32,512]{1,0:T(8,128)(2,1)} %shard.1), custom_call_target="tpu_custom_call" | custom-call | tf_op jit(solution)/shard_map/pallas_call | solution.py:567
  63.4 1.0 %copy.10 = bf16[256,2048]{1,0:T(8,128)(2,1)} copy(bf16[256,2048]{1,0:T(8,128)(2,1)S(1)} %get-tuple-element.2) | data formatting | bytes 2097152
  64.4 0.6 copy.11

commit v8 on v7

--- a/solution.py
+++ b/solution.py
@@ -16,11 +16,11 @@
 HEADS = COLS // HEAD_DIM
 A0, A1 = 384, 512
 F32, BF16 = jnp.float32, jnp.bfloat16
-SENDS, ARRIVALS = 48, 98
+SENDS, ARRIVALS, METER = 8, 98, 1024
 
 
 def kernel(tokens_in, cot, routes, counts, widths, shard, rows_out, grad_out,
-           tokens, W, tokT, dW, proj, dl, D, hot, S, R1, R3, Rf, G, DXs, DXr,
+           meter, tokens, W, tokT, dW, proj, dl, D, hot, S, R1, R3, Rf, G, DXs, DXr,
            aZs, aZr, a1, aYs, aYr, a2, aXs, aXr,
            bXs, bXr, b1, bYs, bYr, cYs, cYr, c1, cXs, cXr, Zf, Zs, Zr,
            local_sem, send_sem, recv_sem):
@@ -41,7 +41,7 @@
         return {"x": device(z, y, j, m), "y": device(z, j, x, m), "z": device(j, y, x, m)}[axis]
 
     partner = device(z, y, x, 1 - m)
-    copies, groups = [], []
+    copies, groups, sent = [], [], [0] * SENDS
 
     class Group:
         def __init__(self, ref):
@@ -50,14 +50,14 @@
 
         def send(self, src, dst, to):
             at = len(copies)
-            if at >= SENDS:
-                copies[at - SENDS].wait_send()
+            size = math.prod(src.shape) * src.dtype.itemsize
             copy = pltpu.make_async_remote_copy(
                 src_ref=src, dst_ref=dst, send_sem=send_sem.at[at % SENDS], recv_sem=self.sem,
                 device_id=to, device_id_type=MESH)
             copy.start()
             copies.append(copy)
-            self.bytes += math.prod(src.shape) * src.dtype.itemsize
+            self.bytes += size
+            sent[at % SENDS] += size
 
         def wait(self):
             assert self.bytes == math.prod(self.ref.shape) * self.ref.dtype.itemsize
@@ -518,8 +518,12 @@
     finish_bc()
     finish_a()
     assert len(groups) == ARRIVALS
-    for copy in copies[-SENDS:]:
-        copy.wait_send()
+    for k in range(SENDS):
+        assert sent[k] % 4096 == 0 and sent[k] <= METER * 4096
+        all_of_them = meter.at[pl.ds(0, sent[k] // 4096)]
+        pltpu.make_async_remote_copy(
+            src_ref=all_of_them, dst_ref=all_of_them, send_sem=send_sem.at[k], recv_sem=recv_sem.at[0],
+            device_id=partner, device_id_type=MESH).wait_send()
 
 
 def per_device(tokens, key_cot, routes, counts, widths, key_weight):
@@ -527,6 +531,7 @@
     smem = pl.BlockSpec(memory_space=pltpu.SMEM)
     anywhere = pl.BlockSpec(memory_space=pl.ANY)
     buffers = [
+        ((METER, 8, 128), F32),
         ((ROWS, WIDTH), BF16),
         ((NZ, NY, NX, FEATS, COLS), BF16),
         ((NZ, SLAB, ROWS), BF16),

time: 65.1 us -> 64.8 us (level)
  no operation moved by 1% of the time
where the time goes in v8:
time: 64.8 us
  Pallas kernels  62.5 us (96%)
  local copies, waits for them, and re-layouts  1.6 us (2%)
    pallas_call x1, Pallas kernels, per_device(): pl.pallas_call(kernel, out_shape=(pltpu.VMEM((2 * ROWS, WIDTH // 2), BF16...  62.5 us
    unnamed x2, local copies, waits for them, and re-layouts  1.6 us

profile of v8, /device:TPU:2, one launch (start us, length us, event | category | flops | bytes accessed | tf_op | source)
XLA Modules:
  0.0 64.8 jit_solution(4020617025405853095)
XLA Ops:
  0.6 62.5 %shard_map.77 = (bf16[256,2048]{1,0:T(8,128)(2,1)S(1)}, f32[32,512]{1,0:T(8,128)S(1)}) custom-call(bf16[128,4096]{1,0:T(8,128)(2,1)} %tokens_in.1, bf16[128,512]{1,0:T(8,128)(2,1)} %cot.1, s32[1,128]{1,0:T(1,128)} %bitcast.1, s32[1,4]{1,0:T(1,128)} %counts.1, s32[4]{0:T(128)} %widths.1, bf16[32,512]{1,0:T(8,128)(2,1)} %shard.1), custom_call_target="tpu_custom_call" | custom-call | tf_op jit(solution)/shard_map/pallas_call | solution.py:572
  63.1 1.0 %copy.10 = bf16[256,2048]{1,0:T(8,128)(2,1)} copy(bf16[256,2048]{1,0:T(8,128)(2,1)S(1)} %get-tuple-element.2) | data formatting | bytes 2097152
  64.1 0.6 copy.11

commit v9 on v8

--- a/solution.py
+++ b/solution.py
@@ -19,8 +19,8 @@
 SENDS, ARRIVALS, METER = 8, 98, 1024
 
 
-def kernel(tokens_in, cot, routes, counts, widths, shard, rows_out, grad_out,
-           meter, tokens, W, tokT, dW, proj, dl, D, hot, S, R1, R3, Rf, G, DXs, DXr,
+def kernel(tokens_in, cot_in, routes_in, counts_in, widths_in, shard, rows_out, grad_out,
+           meter, tokens, cot, routes, counts, widths, W, tokT, dW, proj, dl, D, hot, S, R1, R3, Rf, G, DXs, DXr,
            aZs, aZr, a1, aYs, aYr, a2, aXs, aXr,
            bXs, bXr, b1, bYs, bYr, cYs, cYr, c1, cXs, cXr, Zf, Zs, Zr,
            local_sem, send_sem, recv_sem):
@@ -66,14 +66,18 @@
                 src_ref=self.ref, dst_ref=self.ref, send_sem=send_sem.at[0], recv_sem=self.sem,
                 device_id=partner, device_id_type=MESH).wait_recv()
 
-    fetch = pltpu.make_async_copy(tokens_in, tokens, local_sem.at[0])
-    fetch.start()
+    own_shard = pltpu.make_async_copy(shard, W.at[z, y, x], local_sem.at[0])
+    own_shard.start()
+    fetches = [pltpu.make_async_copy(src, dst, local_sem.at[at + 1]) for at, (src, dst) in enumerate((
+        (routes_in, routes), (counts_in, counts), (widths_in, widths), (cot_in, cot), (tokens_in, tokens)))]
+    for fetch in fetches:
+        fetch.start()
 
     barrier = pltpu.get_barrier_semaphore()
     peers = [along(axis, o) for axis in "xyz" for o in range(1, place[axis][0])] + [partner]
     for peer in peers:
         pl.semaphore_signal(barrier, inc=1, device_id=peer, device_id_type=MESH)
-    W[z, y, x] = shard[...]
+    own_shard.wait()
     pl.semaphore_wait(barrier, len(peers))
 
     up, down = pl.ds(0, 16), pl.ds(16, 16)
@@ -138,6 +142,8 @@
         row = turn("y", -oy)
         ring(a_last[oy], "z", k, lambda j, h: W.at[j, row, span(h), :, ca])
 
+    for fetch in fetches:
+        fetch.wait()
     named = jnp.broadcast_to(routes[...], (ROWS, ROWS))
     first_index = lax.broadcasted_iota(jnp.int32, (ROWS, ROWS), 0)
     second_index = lax.broadcasted_iota(jnp.int32, (ROWS, ROWS), 1)
@@ -365,7 +371,6 @@
             total += aXr[o].astype(F32)
         grad_out[:, A0:A1] = total * scale
 
-    fetch.wait()
     a_row()
     a_far(1, 0)
     prepare(1)
@@ -528,11 +533,12 @@
 
 def per_device(tokens, key_cot, routes, counts, widths, key_weight):
     vmem = pl.BlockSpec(memory_space=pltpu.VMEM)
-    smem = pl.BlockSpec(memory_space=pltpu.SMEM)
     anywhere = pl.BlockSpec(memory_space=pl.ANY)
     buffers = [
         ((METER, 8, 128), F32),
         ((ROWS, WIDTH), BF16),
+        ((ROWS, COLS), BF16),
+        ((1, ROWS), jnp.int32),
         ((NZ, NY, NX, FEATS, COLS), BF16),
         ((NZ, SLAB, ROWS), BF16),
         ((NZ, NY, NX, FEATS, COLS), F32),
@@ -572,10 +578,12 @@
     rows, grad = pl.pallas_call(
         kernel,
         out_shape=(pltpu.VMEM((2 * ROWS, WIDTH // 2), BF16), pltpu.VMEM((FEATS, COLS), F32)),
-        in_specs=[anywhere, vmem, vmem, smem, smem, vmem],
+        in_specs=[anywhere] * 6,
         out_specs=(vmem, vmem),
-        scratch_shapes=[pltpu.VMEM(shape, dtype) for shape, dtype in buffers]
-        + [pltpu.SemaphoreType.DMA((1,)), pltpu.SemaphoreType.DMA((SENDS,)), pltpu.SemaphoreType.DMA((ARRIVALS,))],
+        scratch_shapes=[pltpu.VMEM(shape, dtype) for shape, dtype in buffers[:4]]
+        + [pltpu.SMEM((1, 4), jnp.int32), pltpu.SMEM((4,), jnp.int32)]
+        + [pltpu.VMEM(shape, dtype) for shape, dtype in buffers[4:]]
+        + [pltpu.SemaphoreType.DMA((6,)), pltpu.SemaphoreType.DMA((SENDS,)), pltpu.SemaphoreType.DMA((ARRIVALS,))],
         compiler_params=pltpu.CompilerParams(
             collective_id=0, has_side_effects=True, vmem_limit_bytes=58 << 20),
     )(tokens, key_cot, routes.reshape(1, ROWS), counts, widths, key_weight)

time: 64.8 us -> 64 us (0.988)
  Pallas kernels: 62.5 us -> 61.7 us
    pallas_call x1, Pallas kernels: 62.5 us -> 61.7 us  [per_device(): pl.pallas_call(kernel, out_shape=(pltpu.VMEM((2 * ROWS, WIDTH // 2), BF16...]
where the time goes in v9:
time: 64 us; the launch traced here: 63.9 us
  Pallas kernels  61.7 us (96%)
  local copies, waits for them, and re-layouts  1.6 us (2%)
  between operations  0.64 us (1%)
    pallas_call x1, Pallas kernels, per_device(): pl.pallas_call(kernel, out_shape=(pltpu.VMEM((2 * ROWS, WIDTH // 2), BF16...  61.7 us
    unnamed x2, local copies, waits for them, and re-layouts  1.6 us

profile of v9, /device:TPU:2, one launch (start us, length us, event | category | flops | bytes accessed | tf_op | source)
XLA Modules:
  0.0 63.9 jit_solution(16477771753961405146)
XLA Ops:
  0.6 61.7 %shard_map.77 = (bf16[256,2048]{1,0:T(8,128)(2,1)S(1)}, f32[32,512]{1,0:T(8,128)S(1)}) custom-call(bf16[128,4096]{1,0:T(8,128)(2,1)} %tokens_in.1, bf16[128,512]{1,0:T(8,128)(2,1)} %cot_in.1, s32[1,128]{1,0:T(1,128)} %bitcast.1, s32[1,4]{1,0:T(1,128)} %counts_in.1, s32[4]{0:T(128)} %widths_in.1, bf16[32,512]{1,0:T(8,128)(2,1)} %shard.1), custom_call_target="tpu_custom_call" | custom-call | tf_op jit(solution)/shard_map/pallas_call | solution.py:578
  62.3 1.0 %copy.10 = bf16[256,2048]{1,0:T(8,128)(2,1)} copy(bf16[256,2048]{1,0:T(8,128)(2,1)S(1)} %get-tuple-element.2) | data formatting | bytes 2097152
  63.3 0.6 copy.11

commit v10 on v9

--- a/solution.py
+++ b/solution.py
@@ -66,17 +66,17 @@
                 src_ref=self.ref, dst_ref=self.ref, send_sem=send_sem.at[0], recv_sem=self.sem,
                 device_id=partner, device_id_type=MESH).wait_recv()
 
+    barrier = pltpu.get_barrier_semaphore()
+    peers = [along(axis, o) for axis in "xyz" for o in range(1, place[axis][0])] + [partner]
+    for peer in peers:
+        pl.semaphore_signal(barrier, inc=1, device_id=peer, device_id_type=MESH)
+
     own_shard = pltpu.make_async_copy(shard, W.at[z, y, x], local_sem.at[0])
     own_shard.start()
     fetches = [pltpu.make_async_copy(src, dst, local_sem.at[at + 1]) for at, (src, dst) in enumerate((
         (routes_in, routes), (counts_in, counts), (widths_in, widths), (cot_in, cot), (tokens_in, tokens)))]
     for fetch in fetches:
         fetch.start()
-
-    barrier = pltpu.get_barrier_semaphore()
-    peers = [along(axis, o) for axis in "xyz" for o in range(1, place[axis][0])] + [partner]
-    for peer in peers:
-        pl.semaphore_signal(barrier, inc=1, device_id=peer, device_id_type=MESH)
     own_shard.wait()
     pl.semaphore_wait(barrier, len(peers))
 
@@ -371,66 +371,66 @@
             total += aXr[o].astype(F32)
         grad_out[:, A0:A1] = total * scale
 
+    prepare(2)
     a_row()
+    chunks[0].far(1)
     a_far(1, 0)
-    prepare(1)
+    arrive(3)
+    arrive(5)
+    arrive(1)
+    prepare(7)
+    arrive(2)
     arrive(4)
-    chunks[0].far(1)
-    prepare(4)
-    arrive(5)
-    arrive(3)
-    arrive(2)
-    arrive(1)
+    prepare(5)
     a_far(2, 0)
+    arrive(7)
     arrive(6)
     a_y.wait()
+    a_far(1, 3)
+    chunks[0].far(2)
     a_far(1, 1)
     a_far(1, 2)
-    a_far(1, 3)
-    prepare(5)
-    arrive(7)
-    chunks[0].far(2)
+    chunks[3].far(1)
+    a_far(3, 0)
+    chunks[5].far(1)
+    a_far(2, 3)
+    chunks[2].far(1)
     chunks[4].far(1)
-    chunks[3].far(1)
+    a_far(2, 1)
+    a_far(2, 2)
+    chunks[1].far(1)
+    chunks[6].far(1)
+    chunks[7].far(1)
     prepare(6)
-    a_far(3, 0)
-    a_far(2, 1)
-    chunks[2].far(1)
-    prepare(3)
-    a_far(2, 2)
-    chunks[7].far(1)
-    a_far(2, 3)
-    chunks[1].far(1)
-    a_far(4, 0)
-    chunks[6].far(1)
-    a_far(3, 1)
-    chunks[5].far(1)
-    a_far(3, 2)
     prepare(0)
     a_far(3, 3)
+    chunks[5].far(2)
+    chunks[3].far(2)
+    a_far(3, 1)
+    prepare(4)
     chunks[0].group.wait()
     forward(0)
+    a_far(3, 2)
+    prepare(3)
+    chunks[2].far(2)
+    a_far(4, 0)
+    prepare(1)
+    chunks[1].far(2)
     chunks[4].far(2)
+    chunks[6].far(2)
+    a_far(4, 3)
+    a_far(4, 1)
     chunks[7].far(2)
-    chunks[3].far(2)
-    chunks[1].far(2)
-    a_far(4, 1)
-    chunks[2].far(2)
-    chunks[6].far(2)
     a_far(4, 2)
-    chunks[5].far(2)
-    a_far(4, 3)
-    chunks[4].group.wait()
     chunks[3].group.wait()
     forward(3)
-    prepare(7)
     chunks[2].group.wait()
     forward(2)
-    chunks[7].group.wait()
-    forward(7)
+    chunks[5].group.wait()
+    forward(5)
     chunks[1].group.wait()
     forward(1)
-    prepare(2)
+    chunks[4].group.wait()
     chunks[6].group.wait()
     forward(6)
     a_last[0].wait()
@@ -438,89 +438,89 @@
     a_last[2].wait()
     a_last[3].wait()
     forward(4)
-    chunks[5].group.wait()
-    forward(5)
+    chunks[7].group.wait()
+    forward(7)
     norm_grads()
-    units[6].term()
+    units[7].term()
+    units[7].step(1)
     pack(4)
-    units[6].step(1)
-    units[5].term()
-    units[5].step(1)
     units[0].term()
     units[0].step(1)
-    a_step(1, 2)
-    a_step(1, 3)
+    units[6].term()
+    units[6].step(1)
     units[4].term()
     units[4].step(1)
+    a_step(1, 1)
+    a_step(1, 3)
     units[1].term()
-    a_step(1, 1)
     units[1].step(1)
+    units[5].term()
+    a_step(1, 2)
+    units[5].step(1)
     pack(5)
+    pack(2)
     units[3].term()
     units[3].step(1)
-    pack(3)
     units[2].term()
     units[2].step(1)
-    units[7].term()
-    units[7].step(1)
-    units[6].step(2)
     a_step(1, 0)
-    pack(7)
-    a_step(2, 2)
+    pack(3)
     units[0].step(2)
     a_step(2, 1)
-    units[4].step(2)
+    units[6].step(2)
+    pack(6)
+    units[1].step(2)
+    a_step(2, 2)
+    units[3].step(2)
     a_step(2, 3)
-    pack(6)
-    pack(2)
-    units[2].step(2)
-    units[1].step(2)
     pack(1)
     units[5].step(2)
+    units[2].step(2)
+    pack(7)
+    units[4].step(2)
+    a_step(2, 0)
+    pack(0)
+    units[0].near()
+    a_step(3, 1)
+    a_step(3, 2)
+    units[1].near()
+    a_step(3, 3)
+    route_plane()
+    a_step(3, 0)
     units[6].near()
-    a_step(2, 0)
-    a_step(3, 2)
-    units[0].near()
-    units[3].step(2)
+    a_step(4, 1)
+    a_step(4, 2)
+    units[3].near()
+    a_step(4, 3)
+    units[2].near()
+    units[5].near()
+    a_step(4, 0)
     units[4].near()
-    a_step(3, 1)
-    a_step(3, 3)
-    pack(0)
-    route_plane()
-    units[1].near()
-    a_step(3, 0)
-    units[2].near()
-    a_step(4, 2)
-    a_step(4, 1)
-    units[5].near()
-    a_step(4, 3)
-    units[3].near()
     units[7].step(2)
-    a_step(4, 0)
-    units[4].across()
+    units[0].across()
     a_over_y(2)
+    units[1].across()
     a_over_y(1)
     a_over_y(3)
-    units[0].across()
-    units[1].across()
+    units[6].across()
     unpack()
     units[2].across()
     give(0)
     give(1)
+    units[5].across()
     give(2)
+    units[3].across()
+    units[4].across()
+    units[7].near()
+    a_over_y(0)
     give(3)
-    units[3].across()
-    units[7].near()
-    units[5].across()
-    units[6].across()
-    a_over_y(0)
     a_over_x()
     take(0)
     take(1)
     take(2)
     units[7].across()
+    finish_bc()
     take(3)
-    finish_bc()
     finish_a()
     assert len(groups) == ARRIVALS
     for k in range(SENDS):

time: 64 us -> 62.6 us (0.978)
  Pallas kernels: 61.7 us -> 60.2 us
    pallas_call x1, Pallas kernels: 61.7 us -> 60.2 us  [per_device(): pl.pallas_call(kernel, out_shape=(pltpu.VMEM((2 * ROWS, WIDTH // 2), BF16...]
where the time goes in v10:
time: 62.6 us; the launch traced here: 62.5 us
  Pallas kernels  60.2 us (96%)
  local copies, waits for them, and re-layouts  1.6 us (3%)
  between operations  0.64 us (1%)
    pallas_call x1, Pallas kernels, per_device(): pl.pallas_call(kernel, out_shape=(pltpu.VMEM((2 * ROWS, WIDTH // 2), BF16...  60.2 us
    unnamed x2, local copies, waits for them, and re-layouts  1.6 us

profile of v10, /device:TPU:2, one launch (start us, length us, event | category | flops | bytes accessed | tf_op | source)
XLA Modules:
  0.0 62.5 jit_solution(998397876375567247)
XLA Ops:
  0.6 60.2 %shard_map.77 = (bf16[256,2048]{1,0:T(8,128)(2,1)S(1)}, f32[32,512]{1,0:T(8,128)S(1)}) custom-call(bf16[128,4096]{1,0:T(8,128)(2,1)} %tokens_in.1, bf16[128,512]{1,0:T(8,128)(2,1)} %cot_in.1, s32[1,128]{1,0:T(1,128)} %bitcast.1, s32[1,4]{1,0:T(1,128)} %counts_in.1, s32[4]{0:T(128)} %widths_in.1, bf16[32,512]{1,0:T(8,128)(2,1)} %shard.1), custom_call_target="tpu_custom_call" | custom-call | tf_op jit(solution)/shard_map/pallas_call | solution.py:578
  60.9 1.0 %copy.10 = bf16[256,2048]{1,0:T(8,128)(2,1)} copy(bf16[256,2048]{1,0:T(8,128)(2,1)S(1)} %get-tuple-element.2) | data formatting | bytes 2097152
  61.8 0.6 %copy.11 = f32[32,512]{1,0:T(8,128)} copy(f32[32,512]{1,0:T(8,128)S(1)} %get-tuple-element.3) | data formatting | bytes 131072

commit v11 on v10

--- a/solution.py
+++ b/solution.py
@@ -531,6 +531,21 @@
             device_id=partner, device_id_type=MESH).wait_send()
 
 
+PIECES = 4
+
+
+def hand_on(rows, grad, rows_out, grad_out, sem):
+    copies = [pltpu.make_async_copy(grad, grad_out, sem.at[PIECES])]
+    size = rows.shape[0] // PIECES
+    for i in range(PIECES):
+        part = pl.ds(i * size, size)
+        copies.append(pltpu.make_async_copy(rows.at[part], rows_out.at[part], sem.at[i]))
+    for copy in copies:
+        copy.start()
+    for copy in copies:
+        copy.wait()
+
+
 def per_device(tokens, key_cot, routes, counts, widths, key_weight):
     vmem = pl.BlockSpec(memory_space=pltpu.VMEM)
     anywhere = pl.BlockSpec(memory_space=pl.ANY)
@@ -587,7 +602,13 @@
         compiler_params=pltpu.CompilerParams(
             collective_id=0, has_side_effects=True, vmem_limit_bytes=58 << 20),
     )(tokens, key_cot, routes.reshape(1, ROWS), counts, widths, key_weight)
-    return rows, grad
+    return pl.pallas_call(
+        hand_on,
+        out_shape=(jax.ShapeDtypeStruct(rows.shape, BF16), jax.ShapeDtypeStruct(grad.shape, F32)),
+        in_specs=[vmem, vmem],
+        out_specs=(anywhere, anywhere),
+        scratch_shapes=[pltpu.SemaphoreType.DMA((PIECES + 1,))],
+    )(*(pltpu.with_memory_space_constraint(held, pltpu.VMEM) for held in (rows, grad)))
 
 
 def solution(mesh):

time: 62.6 us -> 62 us (level)
  local copies, waits for them, and re-layouts: 1.6 us -> 0 us
  Pallas kernels: 60.2 us -> 61.2 us
    unnamed x2 -> x0, local copies, waits for them, and re-layouts: 1.6 us -> none
    pallas_call x0 -> x1, Pallas kernels: none -> 1.03 us  [per_device(): pl.pallas_call(hand_on, out_shape=(jax.ShapeDtypeStruct(rows.shape, BF16)...]
where the time goes in v11:
time: 62 us; the launch traced here: 61.9 us
  Pallas kernels  61.2 us (99%)
  between operations  0.64 us (1%)
    pallas_call x1, Pallas kernels, per_device(): pl.pallas_call(kernel, out_shape=(pltpu.VMEM((2 * ROWS, WIDTH // 2), BF16...  60.2 us

profile of v11, /device:TPU:2, one launch (start us, length us, event | category | flops | bytes accessed | tf_op | source)
XLA Modules:
  0.0 61.9 jit_solution(17842624687921642641)
XLA Ops:
  0.6 60.2 %shard_map.77 = (bf16[256,2048]{1,0:T(8,128)(2,1)S(1)}, f32[32,512]{1,0:T(8,128)S(1)}) custom-call(bf16[128,4096]{1,0:T(8,128)(2,1)} %tokens_in.1, bf16[128,512]{1,0:T(8,128)(2,1)} %cot_in.1, s32[1,128]{1,0:T(1,128)} %bitcast.1, s32[1,4]{1,0:T(1,128)} %counts_in.1, s32[4]{0:T(128)} %widths_in.1, bf16[32,512]{1,0:T(8,128)(2,1)} %shard.1), custom_call_target="tpu_custom_call" | custom-call | tf_op jit(solution)/shard_map/pallas_call | solution.py:593
  60.9 1.0 %shard_map.78 = (bf16[256,2048]{1,0:T(8,128)(2,1)}, f32[32,512]{1,0:T(8,128)}) custom-call(bf16[256,2048]{1,0:T(8,128)(2,1)S(1)} %get-tuple-element.4.rows, f32[32,512]{1,0:T(8,128)S(1)} %get-tuple-element.5.grad), custom_call_target="tpu_custom_call" | custom-call | tf_op jit(solution)/shard_map/pallas_call | solution.py:605

commit v12 on v11

--- a/solution.py
+++ b/solution.py
@@ -371,156 +371,156 @@
             total += aXr[o].astype(F32)
         grad_out[:, A0:A1] = total * scale
 
-    prepare(2)
     a_row()
+    prepare(3)
+    a_far(1, 0)
     chunks[0].far(1)
-    a_far(1, 0)
-    arrive(3)
     arrive(5)
     arrive(1)
-    prepare(7)
     arrive(2)
-    arrive(4)
-    prepare(5)
+    arrive(3)
+    arrive(6)
+    prepare(4)
     a_far(2, 0)
     arrive(7)
-    arrive(6)
     a_y.wait()
     a_far(1, 3)
+    arrive(4)
     chunks[0].far(2)
+    a_far(1, 2)
     a_far(1, 1)
-    a_far(1, 2)
+    chunks[5].far(1)
+    chunks[1].far(1)
+    prepare(0)
+    chunks[2].far(1)
+    prepare(5)
     chunks[3].far(1)
-    a_far(3, 0)
-    chunks[5].far(1)
+    prepare(7)
     a_far(2, 3)
-    chunks[2].far(1)
-    chunks[4].far(1)
+    a_far(2, 2)
     a_far(2, 1)
-    a_far(2, 2)
-    chunks[1].far(1)
-    chunks[6].far(1)
     chunks[7].far(1)
     prepare(6)
-    prepare(0)
+    a_far(3, 0)
+    chunks[4].far(1)
+    prepare(1)
+    chunks[6].far(1)
     a_far(3, 3)
-    chunks[5].far(2)
-    chunks[3].far(2)
+    a_far(3, 2)
     a_far(3, 1)
-    prepare(4)
+    prepare(2)
     chunks[0].group.wait()
     forward(0)
-    a_far(3, 2)
-    prepare(3)
+    chunks[3].far(2)
+    chunks[5].far(2)
+    a_far(4, 0)
+    chunks[1].far(2)
     chunks[2].far(2)
-    a_far(4, 0)
-    prepare(1)
-    chunks[1].far(2)
+    a_far(4, 3)
     chunks[4].far(2)
-    chunks[6].far(2)
-    a_far(4, 3)
-    a_far(4, 1)
     chunks[7].far(2)
     a_far(4, 2)
+    a_far(4, 1)
+    chunks[6].far(2)
+    chunks[5].group.wait()
+    forward(5)
     chunks[3].group.wait()
     forward(3)
+    chunks[4].group.wait()
     chunks[2].group.wait()
     forward(2)
-    chunks[5].group.wait()
-    forward(5)
     chunks[1].group.wait()
     forward(1)
-    chunks[4].group.wait()
-    chunks[6].group.wait()
-    forward(6)
+    chunks[7].group.wait()
+    forward(7)
     a_last[0].wait()
     a_last[1].wait()
     a_last[2].wait()
     a_last[3].wait()
     forward(4)
-    chunks[7].group.wait()
-    forward(7)
+    chunks[6].group.wait()
+    forward(6)
     norm_grads()
-    units[7].term()
-    units[7].step(1)
+    units[0].term()
+    a_step(1, 2)
+    units[0].step(1)
+    a_step(1, 3)
+    units[2].term()
+    units[2].step(1)
     pack(4)
-    units[0].term()
-    units[0].step(1)
-    units[6].term()
-    units[6].step(1)
     units[4].term()
     units[4].step(1)
+    units[5].term()
+    units[5].step(1)
     a_step(1, 1)
-    a_step(1, 3)
     units[1].term()
     units[1].step(1)
-    units[5].term()
-    a_step(1, 2)
-    units[5].step(1)
     pack(5)
     pack(2)
     units[3].term()
     units[3].step(1)
-    units[2].term()
-    units[2].step(1)
+    units[7].term()
+    units[7].step(1)
+    units[6].term()
+    units[6].step(1)
     a_step(1, 0)
+    a_step(2, 3)
+    units[0].step(2)
+    units[2].step(2)
+    a_step(2, 2)
     pack(3)
-    units[0].step(2)
+    units[4].step(2)
     a_step(2, 1)
+    units[5].step(2)
+    pack(1)
+    pack(6)
     units[6].step(2)
-    pack(6)
     units[1].step(2)
-    a_step(2, 2)
+    pack(7)
+    a_step(2, 0)
     units[3].step(2)
-    a_step(2, 3)
-    pack(1)
-    units[5].step(2)
-    units[2].step(2)
-    pack(7)
-    units[4].step(2)
-    a_step(2, 0)
     pack(0)
+    a_step(3, 2)
+    a_step(3, 3)
     units[0].near()
     a_step(3, 1)
-    a_step(3, 2)
+    units[2].near()
+    route_plane()
+    units[4].near()
+    a_step(3, 0)
+    a_step(4, 2)
+    a_step(4, 3)
+    units[3].near()
+    a_step(4, 1)
     units[1].near()
-    a_step(3, 3)
-    route_plane()
-    a_step(3, 0)
     units[6].near()
-    a_step(4, 1)
-    a_step(4, 2)
-    units[3].near()
-    a_step(4, 3)
-    units[2].near()
     units[5].near()
     a_step(4, 0)
-    units[4].near()
+    units[2].across()
     units[7].step(2)
+    a_over_y(2)
     units[0].across()
-    a_over_y(2)
+    a_over_y(3)
+    a_over_y(1)
+    unpack()
+    give(0)
     units[1].across()
-    a_over_y(1)
-    a_over_y(3)
+    units[3].across()
     units[6].across()
-    unpack()
-    units[2].across()
-    give(0)
+    a_over_y(0)
     give(1)
     units[5].across()
+    units[4].across()
     give(2)
-    units[3].across()
-    units[4].across()
+    give(3)
     units[7].near()
-    a_over_y(0)
-    give(3)
     a_over_x()
     take(0)
     take(1)
     take(2)
+    take(3)
     units[7].across()
     finish_bc()
-    take(3)
     finish_a()
     assert len(groups) == ARRIVALS
     for k in range(SENDS):

time: 62 us -> 64.4 us (1.039)
  Pallas kernels: 61.2 us -> 63.5 us
    pallas_call x1, Pallas kernels: 60.2 us -> 62.4 us  [per_device(): pl.pallas_call(kernel, out_shape=(pltpu.VMEM((2 * ROWS, WIDTH // 2), BF16...]
where the time goes in v12:
time: 64.4 us; the launch traced here: 64.1 us
  Pallas kernels  63.5 us (99%)
    pallas_call x1, Pallas kernels, per_device(): pl.pallas_call(kernel, out_shape=(pltpu.VMEM((2 * ROWS, WIDTH // 2), BF16...  62.4 us

profile of v12, /device:TPU:2, one launch (start us, length us, event | category | flops | bytes accessed | tf_op | source)
XLA Modules:
  0.0 64.1 jit_solution(8357053552729545600)
XLA Ops:
  0.6 62.4 %shard_map.77 = (bf16[256,2048]{1,0:T(8,128)(2,1)S(1)}, f32[32,512]{1,0:T(8,128)S(1)}) custom-call(bf16[128,4096]{1,0:T(8,128)(2,1)} %tokens_in.1, bf16[128,512]{1,0:T(8,128)(2,1)} %cot_in.1, s32[1,128]{1,0:T(1,128)} %bitcast.1, s32[1,4]{1,0:T(1,128)} %counts_in.1, s32[4]{0:T(128)} %widths_in.1, bf16[32,512]{1,0:T(8,128)(2,1)} %shard.1), custom_call_target="tpu_custom_call" | custom-call | tf_op jit(solution)/shard_map/pallas_call | solution.py:593
  63.1 1.0 %shard_map.78 = (bf16[256,2048]{1,0:T(8,128)(2,1)}, f32[32,512]{1,0:T(8,128)}) custom-call(bf16[256,2048]{1,0:T(8,128)(2,1)S(1)} %get-tuple-element.4.rows, f32[32,512]{1,0:T(8,128)S(1)} %get-tuple-element.5.grad), custom_call_target="tpu_custom_call" | custom-call | tf_op jit(solution)/shard_map/pallas_call | solution.py:605
